TPU v7x, 512 devices: a whole 4x8x8 slice. The times are simulated.
512 devices in a mesh: slab: 4 (over x), cout: 8 (over y), cin: 16 (over z, core).
Axes of the slice: x: 4, y: 8, z: 8, core: 2. Of those that a mesh axis runs over, the one named last changes fastest.
Arguments:
- image_in: float32 [32, 64, 2048], P('slab', None, 'cin'), may hold values from -6 to 6
- first_weight: float32 [3, 3, 2048, 2048], P(None, None, 'cin', 'cout'), may hold values from -0.046875 to 0.046875
- second_weight: float32 [3, 3, 2048, 2048], P(None, None, 'cout', 'cin'), may hold values from -0.046875 to 0.046875
- out_grad: float32 [32, 64, 2048], P('slab', None, 'cin'), may hold values from -0.13258252 to 0.13258252
Outputs:
- output: float32 [32, 64, 2048], P('slab', 'cout', 'cin')
- weight_grad: float32 [3, 3, 2048, 2048], P(None, None, ('cout', 'slab'), 'cin')
All inputs are finite; a program needn't handle non-finite values.
Results may differ from a plain program's by a relative error of at most 0.0001.
Values sent between devices are 32-bit elements; how exact they have to be, the bound alone decides.
No kernel may reach another device: no remote copies, remote signals or barrier semaphores. Data moves between devices by JAX's collectives and lax.ppermute only.
A program may use at most 64 MiB of HBM per device.

v0:
```python
import jax
import jax.numpy as jnp
from jax import lax
from jax.sharding import PartitionSpec as P


def with_halo(cells, sides, width):
    for axis, dim in sides:
        count = lax.axis_size(axis)
        ends = count - 1
        head = lax.slice_in_dim(cells, 0, width, axis=dim)
        tail = lax.slice_in_dim(cells, cells.shape[dim] - width, cells.shape[dim], axis=dim)
        cells = jnp.concatenate(
            [
                lax.ppermute(tail, axis, [(i, (i + 1) % count) for i in range(ends)]),
                cells,
                lax.ppermute(head, axis, [((i + 1) % count, i) for i in range(ends)]),
            ],
            axis=dim,
        )
    return cells


def conv_taps(padded, weight, row_count, col_count):
    summed = jnp.zeros((row_count * col_count, weight.shape[3]), jnp.float32)
    for row_off in range(3):
        for col_off in range(3):
            window = padded[
                row_off : row_off + row_count, col_off : col_off + col_count, :
            ].reshape(row_count * col_count, -1)
            summed = summed + jnp.dot(
                window,
                weight[row_off, col_off],
                precision=lax.Precision.HIGHEST,
                preferred_element_type=jnp.float32,
            )
    return summed.reshape(row_count, col_count, -1)


def on_device(image_in, first_weight, second_weight, out_grad):
    row_count = image_in.shape[0]
    col_count = image_in.shape[1]
    image_ext = with_halo(image_in, (("slab", 0),), 1)
    padded = jnp.pad(image_ext, ((0, 0), (1, 1), (0, 0)))
    partial_value = conv_taps(padded, first_weight, row_count, col_count)
    hidden = jax.nn.silu(lax.psum(partial_value, "cin"))
    hidden_ext = with_halo(hidden, (("slab", 0),), 1)
    hidden_pad = jnp.pad(hidden_ext, ((0, 0), (1, 1), (0, 0)))
    second_part = conv_taps(hidden_pad, second_weight, row_count, col_count)
    output = lax.psum_scatter(second_part, "cout", scatter_dimension=1, tiled=True)
    flat_grad = out_grad.reshape(row_count * col_count, -1)
    grads = []
    for row_off in range(3):
        for col_off in range(3):
            window = hidden_pad[
                row_off : row_off + row_count, col_off : col_off + col_count, :
            ].reshape(row_count * col_count, -1)
            grads.append(
                lax.dot_general(
                    window,
                    flat_grad,
                    (((0,), (0,)), ((), ())),
                    precision=lax.Precision.HIGHEST,
                    preferred_element_type=jnp.float32,
                )
            )
    local_grad = jnp.stack(grads).reshape(3, 3, hidden.shape[2], flat_grad.shape[1])
    weight_grad = lax.psum_scatter(local_grad, "slab", scatter_dimension=2, tiled=True)
    return (output, weight_grad)


def solution(mesh):
    in_specs = (
        P("slab", None, "cin"),
        P(None, None, "cin", "cout"),
        P(None, None, "cout", "cin"),
        P("slab", None, "cin"),
    )
    out_specs = (P("slab", "cout", "cin"), P(None, None, ("cout", "slab"), "cin"))
    return jax.shard_map(
        on_device, mesh=mesh, in_specs=in_specs, out_specs=out_specs, check_vma=False
    )
```

profile of v0, /device:TPU:6, one launch (start us, length us, event | category | flops | bytes accessed | tf_op | source)
XLA Modules:
  0.0 239.7 jit_solution(1170325807144729229)
XLA Ops:
  8.0 2.7 %collective-permute-start.1 = (f32[1,64,128]{2,1,0:T(8,128)S(1)}, f32[1,64,128]{2,1,0:T(8,128)S(1)}, u32[]{:S(2)}, u32[]{:S(2)}) collective-permute-start(f32[1,64,128]{2,1,0:T(8,128)S(1)} %get-tuple-element.21), channel_id=1, source_target_pairs={{128,0},{256,128},{384,256},{129,1},{257,129},{385,257},{130,2},{2... | collective-permute-start | bytes 98312 | tf_op jit(solution)/shard_map/ppermute | solution.py:17
  10.8 1.3 collective-permute-start
  12.3 4.2 %collective-permute-done = f32[1,64,128]{2,1,0:T(8,128)S(1)} collective-permute-done((f32[1,64,128]{2,1,0:T(8,128)S(1)}, f32[1,64,128]{2,1,0:T(8,128)S(1)}, u32[]{:S(2)}, u32[]{:S(2)}) %collective-permute-start) | collective-permute-done | bytes 32800 | tf_op jit(solution)/shard_map/ppermute | solution.py:15
  16.6 1.0 select_maximum_fusion.2
  17.7 1.1 copy-done.4
  23.5 1.4 fusion
  24.9 121.2 %all-reduce.4.cloned.1.call-done = f32[8,64,256]{2,1,0:T(8,128)} async-done(((f32[8,64,256]{2,1,0:T(8,128)}), f32[8,64,256]{2,1,0:T(8,128)}) %all-reduce.4.cloned.1.call-update) | async-done | bytes 524304 | tf_op jit(solution)/shard_map/psum | solution.py:46
  146.2 1.2 divide_multiply_fusion
  147.4 2.8 %collective-permute-start.3 = (f32[1,64,256]{2,1,0:T(8,128)S(1)}, f32[1,64,256]{2,1,0:T(8,128)S(1)}, u32[]{:S(2)}, u32[]{:S(2)}) collective-permute-start(f32[1,64,256]{2,1,0:T(8,128)S(1)} %get-tuple-element.11), channel_id=1, source_target_pairs={{128,0},{256,128},{384,256},{129,1},{257,129},{385,257},{130,2},{2... | collective-permute-start | bytes 196616 | tf_op jit(solution)/shard_map/ppermute | solution.py:17
  150.1 1.3 collective-permute-start.2
  152.0 4.3 %collective-permute-done.2 = f32[1,64,256]{2,1,0:T(8,128)S(1)} collective-permute-done((f32[1,64,256]{2,1,0:T(8,128)S(1)}, f32[1,64,256]{2,1,0:T(8,128)S(1)}, u32[]{:S(2)}, u32[]{:S(2)}) %collective-permute-start.2) | collective-permute-done | bytes 65568 | tf_op jit(solution)/shard_map/ppermute | solution.py:15
  162.5 1.3 fusion.1
  164.0 1.0 fusion.10
  165.1 1.0 fusion.3
  166.1 1.0 fusion.9
  167.1 1.0 fusion.8
  168.1 1.0 fusion.7
  169.1 1.0 fusion.6
  170.1 1.0 fusion.5
  171.1 1.0 fusion.2
  172.1 1.0 fusion.4
  173.1 1.0 copy-done.2
  174.1 28.8 %reduce-scatter.3.cloned.1.call-done = f32[8,8,128]{2,1,0:T(8,128)} async-done(((f32[8,64,128]{2,1,0:T(8,128)}), f32[8,8,128]{2,1,0:T(8,128)}) %reduce-scatter.3.cloned.1.call-update) | async-done | bytes 32784 | tf_op jit(solution)/shard_map/reduce_scatter | solution.py:50
  203.0 30.1 %reduce-scatter.5.cloned.1.call-done = f32[3,3,64,128]{3,2,1,0:T(8,128)} async-done(((f32[3,3,256,128]{3,2,1,0:T(8,128)}), f32[3,3,64,128]{3,2,1,0:T(8,128)}) %reduce-scatter.5.cloned.1.call-update) | async-done | bytes 294928 | tf_op jit(solution)/shard_map/reduce_scatter | solution.py:68
  (41 shorter events, 12.9 us)
Async XLA Ops:
  7.2 156.9 %copy-start = (f32[8,64,128]{2,1,0:T(8,128)S(1)}, f32[8,64,128]{2,1,0:T(8,128)}, u32[]{:S(2)}) copy-start(f32[8,64,128]{2,1,0:T(8,128)} %param.7) | copy-start | bytes 786436
  7.2 139.0 %all-reduce.4.cloned.1.call-start = ((), (), s32[]{:S(2)}) async-start(), calls=%async_computation.2 | async-start | bytes 1048576 | tf_op jit(solution)/shard_map/psum | solution.py:46
  8.0 4.3 %collective-permute-start.1 = (f32[1,64,128]{2,1,0:T(8,128)S(1)}, f32[1,64,128]{2,1,0:T(8,128)S(1)}, u32[]{:S(2)}, u32[]{:S(2)}) collective-permute-start(f32[1,64,128]{2,1,0:T(8,128)S(1)} %get-tuple-element.21), channel_id=1, source_target_pairs={{128,0},{256,128},{384,256},{129,1},{257,129},{385,257},{130,2},{2... | collective-permute-start | bytes 98312 | tf_op jit(solution)/shard_map/ppermute | solution.py:17
  10.8 5.8 %collective-permute-start = (f32[1,64,128]{2,1,0:T(8,128)S(1)}, f32[1,64,128]{2,1,0:T(8,128)S(1)}, u32[]{:S(2)}, u32[]{:S(2)}) collective-permute-start(f32[1,64,128]{2,1,0:T(8,128)S(1)} %get-tuple-element.20), channel_id=1, source_target_pairs={{0,128},{128,256},{256,384},{1,129},{129,257},{257,385},{2,130},{1... | collective-permute-start | bytes 98312 | tf_op jit(solution)/shard_map/ppermute | solution.py:15
  17.6 1.3 copy-start.4
  17.7 2.3 copy-start.1
  24.9 178.1 %reduce-scatter.3.cloned.1.call-start = ((), (), s32[]{:S(2)}) async-start(), calls=%async_computation.3 | async-start | bytes 294912 | tf_op jit(solution)/shard_map/reduce_scatter | solution.py:50
  147.4 4.7 %collective-permute-start.3 = (f32[1,64,256]{2,1,0:T(8,128)S(1)}, f32[1,64,256]{2,1,0:T(8,128)S(1)}, u32[]{:S(2)}, u32[]{:S(2)}) collective-permute-start(f32[1,64,256]{2,1,0:T(8,128)S(1)} %get-tuple-element.11), channel_id=1, source_target_pairs={{128,0},{256,128},{384,256},{129,1},{257,129},{385,257},{130,2},{2... | collective-permute-start | bytes 196616 | tf_op jit(solution)/shard_map/ppermute | solution.py:17
  150.1 6.2 %collective-permute-start.2 = (f32[1,64,256]{2,1,0:T(8,128)S(1)}, f32[1,64,256]{2,1,0:T(8,128)S(1)}, u32[]{:S(2)}, u32[]{:S(2)}) collective-permute-start(f32[1,64,256]{2,1,0:T(8,128)S(1)} %get-tuple-element.10), channel_id=1, source_target_pairs={{0,128},{128,256},{256,384},{1,129},{129,257},{257,385},{2,130},{1... | collective-permute-start | bytes 196616 | tf_op jit(solution)/shard_map/ppermute | solution.py:15
  156.4 1.3 copy-start.3
  163.8 69.3 %reduce-scatter.5.cloned.1.call-start = ((), (), s32[]{:S(2)}) async-start(), calls=%async_computation.4 | async-start | bytes 1474560 | tf_op jit(solution)/shard_map/reduce_scatter | solution.py:68
  165.0 3.0 %copy-start.5 = (f32[8,64,256]{2,1,0:T(8,128)S(1)}, f32[8,64,256]{2,1,0:T(8,128)}, u32[]{:S(2)}) copy-start(f32[8,64,256]{2,1,0:T(8,128)} %all-reduce.4.cloned.1.call-done) | copy-start | bytes 1572868
  173.1 1.0 copy-start.2
Sparse Core Ops, SparseCore 0:
  25.0 121.1 all-reduce.3
  163.9 39.0 reduce-scatter.2
  206.4 26.6 reduce-scatter.4
where the time goes:
time: 242 us; the launch traced here: 240 us
  waiting for transfers between devices  190 us (79%)
  matrix products  20.8 us (9%)
  between operations  14.1 us (6%)
  starting transfers between devices  8.37 us (3%)
  local copies, waits for them, and re-layouts  4.37 us (2%)
    psum x1, waiting for transfers between devices, on_device(): hidden = jax.nn.silu(lax.psum(partial_value, 'cin'))  121 us
    reduce_scatter x1, waiting for transfers between devices, on_device(): lax.psum_scatter(local_grad, 'slab', scatter_dimension=2, tiled=True)  30.1 us
    reduce_scatter x1, waiting for transfers between devices, on_device(): lax.psum_scatter(second_part, 'cout', scatter_dimension=1, tiled=True)  28.8 us
    dot_general x18, matrix products, conv_taps(): jnp.dot(window, weight[row_off, col_off], precision=lax.Precision.HIGHEST...  11.8 us
    dot_general x9, matrix products, on_device(): lax.dot_general(window, flat_grad, (((0,), (0,)), ((), ())), precision=la...  8.99 us
    ppermute x2, waiting for transfers between devices, with_halo(): lax.ppermute(tail, axis, [(i, (i + 1) % count) for i in range(ends)])  8.5 us
    ppermute x2, starting transfers between devices, with_halo(): lax.ppermute(head, axis, [((i + 1) % count, i) for i in range(ends)])  5.48 us
  transfers between devices with their start and end apart: 7, of which 7 were waited for; matrix products, arithmetic and copies ran while one was open for 4% of the time, Pallas kernels for 0%

commit v1 on v0

v1 whole, which is shorter than its diff:
```python
import jax
import jax.numpy as jnp
from jax import lax
from jax.sharding import PartitionSpec as P

HIGH = lax.Precision.HIGH


def shift(value, axis, step, wrap):
    count = lax.axis_size(axis)
    pairs = [(i, (i + step) % count) for i in range(count) if wrap or 0 <= i + step < count]
    return lax.ppermute(value, axis, pairs)


def conv_taps(padded, weight, row_count, col_count):
    summed = None
    for row_off in range(3):
        for col_off in range(3):
            window = padded[
                row_off : row_off + row_count, col_off : col_off + col_count, :
            ].reshape(row_count * col_count, -1)
            part = jnp.dot(
                window,
                weight[row_off, col_off],
                precision=HIGH,
                preferred_element_type=jnp.float32,
            )
            summed = part if summed is None else summed + part
    return summed


def on_device(image_in, first_weight, second_weight, out_grad):
    rows, cols = image_in.shape[0], image_in.shape[1]
    slabs, n_in, n_out = lax.axis_size("slab"), lax.axis_size("cin"), lax.axis_size("cout")
    slab = lax.axis_index("slab")
    ext_rows = rows + 2

    above = shift(image_in[rows - 2 :], "slab", 1, False)
    below = shift(image_in[:2], "slab", -1, False)
    image_ext = jnp.concatenate([above, image_in, below], axis=0)
    padded = jnp.pad(image_ext, ((0, 0), (1, 1), (0, 0)))
    partial_value = conv_taps(padded, first_weight, ext_rows, cols)

    mid = partial_value.shape[1]
    chunk = ext_rows * cols // n_in
    pieces = lax.all_to_all(
        partial_value.reshape(n_in, chunk, mid), "cin", 0, 0, tiled=True
    )
    own = jax.nn.silu(jnp.sum(pieces, axis=0))
    hidden_ext = lax.all_gather(own, "cin", axis=0, tiled=True).reshape(ext_rows, cols, mid)
    row_at = slab * rows - 1 + jnp.arange(ext_rows)
    inside = (row_at >= 0) & (row_at < slabs * rows)
    hidden_ext = jnp.where(inside[:, None, None], hidden_ext, 0.0)
    hidden_pad = jnp.pad(hidden_ext, ((0, 0), (1, 1), (0, 0)))

    flat_grad = out_grad.reshape(rows * cols, -1)
    grads = []
    for row_off in range(3):
        for col_off in range(3):
            window = hidden_pad[
                row_off : row_off + rows, col_off : col_off + cols, :
            ].reshape(rows * cols, -1)
            grads.append(
                lax.dot_general(
                    window,
                    flat_grad,
                    (((0,), (0,)), ((), ())),
                    precision=HIGH,
                    preferred_element_type=jnp.float32,
                )
            )
    local_grad = jnp.stack(grads)
    part = mid // slabs
    kept = lax.dynamic_slice_in_dim(local_grad, slab * part, part, axis=1)
    for step in range(1, slabs):
        sent = lax.dynamic_slice_in_dim(
            local_grad, lax.rem(slab + step, slabs) * part, part, axis=1
        )
        kept = kept + shift(sent, "slab", step, True)
    weight_grad = kept.reshape(3, 3, part, flat_grad.shape[1])

    second_part = conv_taps(hidden_pad, second_weight, rows, cols)
    second_part = second_part.reshape(rows, n_out, cols // n_out, -1).transpose(1, 0, 2, 3)
    gathered = lax.all_to_all(second_part, "cout", 0, 0, tiled=True)
    output = jnp.sum(gathered, axis=0)
    return (output, weight_grad)


def solution(mesh):
    in_specs = (
        P("slab", None, "cin"),
        P(None, None, "cin", "cout"),
        P(None, None, "cout", "cin"),
        P("slab", None, "cin"),
    )
    out_specs = (P("slab", "cout", "cin"), P(None, None, ("cout", "slab"), "cin"))
    return jax.shard_map(
        on_device, mesh=mesh, in_specs=in_specs, out_specs=out_specs, check_vma=False
    )
```

time: 242 us -> 104 us (0.43)
  waiting for transfers between devices: 190 us -> 29.9 us
  starting transfers between devices: 8.37 us -> 35.1 us
  blocking collectives: 0 us -> 18 us
  between operations: 14.1 us -> 0.98 us
  matrix products: 20.8 us -> 13.3 us
    psum x1 -> x0, waiting for transfers between devices: 121 us -> none  [on_device(): hidden = jax.nn.silu(lax.psum(partial_value, 'cin'))]
    reduce_scatter x2 -> x0, waiting for transfers between devices: 59 us -> none  [the longest x1 30.1 us: on_device(): lax.psum_scatter(local_grad, 'slab', scatter_dimension=2, tiled=True)]
    all_to_all x0 -> x2, waiting for transfers between devices: none -> 29 us  [the longest x1 18.2 us: on_device(): lax.all_to_all(partial_value.reshape(n_in, chunk, mid), 'cin', 0, 0, tile...]
    all_gather x0 -> x1, blocking collectives: none -> 18 us  [on_device(): lax.all_gather(own, 'cin', axis=0, tiled=True).reshape(ext_rows, cols, mid)]
    all_to_all x0 -> x2, starting transfers between devices: none -> 17.5 us  [the longest x1 10.4 us: on_device(): lax.all_to_all(partial_value.reshape(n_in, chunk, mid), 'cin', 0, 0, tile...]
    ppermute x4 -> x5, starting transfers between devices: 8.06 us -> 17.6 us  [shift(): return lax.ppermute(value, axis, pairs)]
    ppermute x4 -> x5, waiting for transfers between devices: 9.37 us -> 0.92 us  [shift(): return lax.ppermute(value, axis, pairs)]
    dot_general x27, matrix products: 20.8 us -> 13.3 us  [the longest x18 7.98 us: conv_taps(): jnp.dot(window, weight[row_off, col_off], precision=HIGH, preferred_eleme...]
  transfers between devices with their start and end apart: 7 -> 7, of which waited for: 7 -> 4; matrix products, arithmetic and copies ran while one was open for 4% -> 6% of each run, Pallas kernels for 0% -> 0%
where the time goes in v1:
time: 104 us; the launch traced here: 103 us
  starting transfers between devices  35.1 us (34%)
  waiting for transfers between devices  29.9 us (29%)
  blocking collectives  18 us (17%)
  matrix products  13.3 us (13%)
  local copies, waits for them, and re-layouts  4.49 us (4%)
  other arithmetic  1.66 us (2%)
    all_to_all x1, waiting for transfers between devices, on_device(): lax.all_to_all(partial_value.reshape(n_in, chunk, mid), 'cin', 0, 0, tile...  18.2 us
    all_gather x1, blocking collectives, on_device(): lax.all_gather(own, 'cin', axis=0, tiled=True).reshape(ext_rows, cols, mid)  18 us
    ppermute x5, starting transfers between devices, shift(): return lax.ppermute(value, axis, pairs)  17.6 us
    all_to_all x1, waiting for transfers between devices, on_device(): gathered = lax.all_to_all(second_part, 'cout', 0, 0, tiled=True)  10.7 us
    all_to_all x1, starting transfers between devices, on_device(): lax.all_to_all(partial_value.reshape(n_in, chunk, mid), 'cin', 0, 0, tile...  10.4 us
    dot_general x18, matrix products, conv_taps(): jnp.dot(window, weight[row_off, col_off], precision=HIGH, preferred_eleme...  7.98 us
    all_to_all x1, starting transfers between devices, on_device(): gathered = lax.all_to_all(second_part, 'cout', 0, 0, tiled=True)  7.11 us
    dot_general x9, matrix products, on_device(): lax.dot_general(window, flat_grad, (((0,), (0,)), ((), ())), precision=HI...  5.36 us
  transfers between devices with their start and end apart: 7, of which 4 were waited for; matrix products, arithmetic and copies ran while one was open for 6% of the time, Pallas kernels for 0%

profile of v1, /device:TPU:6, one launch (start us, length us, event | category | flops | bytes accessed | tf_op | source)
XLA Modules:
  0.0 103.5 jit_solution(9488094119486492293)
XLA Ops:
  0.6 0.9 fusion.51
  1.6 1.3 %collective-permute-start = (f32[2,64,128]{2,1,0:T(8,128)S(1)}, f32[2,64,128]{2,1,0:T(8,128)S(1)}, u32[]{:S(2)}, u32[]{:S(2)}) collective-permute-start(f32[2,64,128]{2,1,0:T(8,128)S(1)} %get-tuple-element.24), channel_id=1, source_target_pairs={{0,128},{128,256},{256,384},{1,129},{129,257},{257,385},{2,130},{1... | collective-permute-start | bytes 196616 | tf_op jit(solution)/shard_map/ppermute | solution.py:12
  2.9 4.5 %collective-permute-start.1 = (f32[2,64,128]{2,1,0:T(8,128)S(1)}, f32[2,64,128]{2,1,0:T(8,128)S(1)}, u32[]{:S(2)}, u32[]{:S(2)}) collective-permute-start(f32[2,64,128]{2,1,0:T(8,128)S(1)} %get-tuple-element.23), channel_id=1, source_target_pairs={{128,0},{256,128},{384,256},{129,1},{257,129},{385,257},{130,2},{2... | collective-permute-start | bytes 196616 | tf_op jit(solution)/shard_map/ppermute | solution.py:12
  7.7 1.0 constant_dynamic-update-slice_fusion.1
  8.7 0.6 collective-permute-done.1
  9.6 1.0 copy-done.2
  14.0 1.3 %fusion = f32[640,256]{1,0:T(8,128)} fusion(f32[640,256]{1,0:T(8,128)S(1)} %fusion.21, f32[640,256]{1,0:T(8,128)S(1)} %convolution_add_fusion.1, f32[640,128]{1,0:T(8,128)S(1)} %bitcast.169, f32[3,3,128,256]{3,2,1,0:T(8,128)S(1)} %copy-done.2), kind=kOutput, calls=%fused_computation.1 | convolution fusion | flops 126156800 | bytes 2424832 | tf_op jit(solution)/shard_map/dot_general | solution.py:22
  15.3 10.4 %all-to-all-start = ((f32[16,40,256]{2,1,0:T(8,128)}), f32[16,40,256]{2,1,0:T(8,128)S(1)}, u32[]{:S(2)}, u32[]{:S(2)}) async-start(f32[16,40,256]{2,1,0:T(8,128)} %bitcast.18), calls=%async_computation | async-start | bytes 1310720 | tf_op jit(solution)/shard_map/all_to_all | solution.py:46
  25.7 18.2 %all-to-all-done = f32[16,40,256]{2,1,0:T(8,128)S(1)} async-done(((f32[16,40,256]{2,1,0:T(8,128)}), f32[16,40,256]{2,1,0:T(8,128)S(1)}, u32[]{:S(2)}, u32[]{:S(2)}) %all-to-all-start) | async-done | bytes 655392 | tf_op jit(solution)/shard_map/all_to_all | solution.py:46
  44.0 18.0 %all_gather.3 = f32[640,256]{1,0:T(8,128)S(1)} all-gather(f32[40,256]{1,0:T(8,128)S(1)} %divide_multiply_fusion), channel_id=1, replica_groups=mesh['slab'=4,'cout'=8,'cin'=16] {'cin'}, dimensions={0}, use_global_device_ids=true | all-gather | bytes 696320 | tf_op jit(solution)/shard_map/all_gather | solution.py:50
  62.7 0.6 fusion.10
  63.9 0.6 fusion.9
  64.5 0.6 fusion.8
  65.7 0.6 fusion.7
  66.3 0.6 fusion.6
  67.5 0.6 fusion.5
  68.2 4.3 %collective-permute-start.4 = (f32[9,64,128]{2,1,0:T(8,128)S(1)}, f32[9,64,128]{2,1,0:T(8,128)S(1)}, u32[]{:S(2)}, u32[]{:S(2)}) collective-permute-start(f32[9,64,128]{2,1,0:T(8,128)S(1)} %get-tuple-element.3), channel_id=1, source_target_pairs={{0,384},{128,0},{256,128},{384,256},{1,385},{129,1},{257,129},{385... | collective-permute-start | bytes 884744 | tf_op jit(solution)/shard_map/ppermute | solution.py:12
  72.5 3.3 %collective-permute-start.3 = (f32[9,64,128]{2,1,0:T(8,128)S(1)}, f32[9,64,128]{2,1,0:T(8,128)S(1)}, u32[]{:S(2)}, u32[]{:S(2)}) collective-permute-start(f32[9,64,128]{2,1,0:T(8,128)S(1)} %get-tuple-element.4), channel_id=1, source_target_pairs={{0,256},{128,384},{256,0},{384,128},{1,257},{129,385},{257,1},{385... | collective-permute-start | bytes 884744 | tf_op jit(solution)/shard_map/ppermute | solution.py:12
  75.8 4.2 %collective-permute-start.2 = (f32[9,64,128]{2,1,0:T(8,128)S(1)}, f32[9,64,128]{2,1,0:T(8,128)S(1)}, u32[]{:S(2)}, u32[]{:S(2)}) collective-permute-start(f32[9,64,128]{2,1,0:T(8,128)S(1)} %get-tuple-element.2), channel_id=1, source_target_pairs={{0,128},{128,256},{256,384},{384,0},{1,129},{129,257},{257,385},{3... | collective-permute-start | bytes 884744 | tf_op jit(solution)/shard_map/ppermute | solution.py:12
  83.5 0.7 copy.8
  84.2 7.1 %all-to-all-start.1 = ((f32[8,8,8,128]{3,2,1,0:T(8,128)}), f32[8,8,8,128]{3,2,1,0:T(8,128)S(1)}, u32[]{:S(2)}, u32[]{:S(2)}) async-start(f32[8,8,8,128]{3,2,1,0:T(8,128)} %bitcast.153), calls=%async_computation.1 | async-start | bytes 524288 | tf_op jit(solution)/shard_map/all_to_all | solution.py:84
  91.3 0.8 add_add_fusion
  92.1 10.7 %all-to-all-done.1 = f32[8,8,8,128]{3,2,1,0:T(8,128)S(1)} async-done(((f32[8,8,8,128]{3,2,1,0:T(8,128)}), f32[8,8,8,128]{3,2,1,0:T(8,128)S(1)}, u32[]{:S(2)}, u32[]{:S(2)}) %all-to-all-start.1) | async-done | bytes 262176 | tf_op jit(solution)/shard_map/all_to_all | solution.py:84
  102.9 0.6 reduce_sum.19
  (41 shorter events, 9.9 us)
Async XLA Ops:
  0.6 62.0 %copy-start = (f32[8,64,128]{2,1,0:T(8,128)S(1)}, f32[8,64,128]{2,1,0:T(8,128)}, u32[]{:S(2)}) copy-start(f32[8,64,128]{2,1,0:T(8,128)} %param.7) | copy-start | bytes 786436
  1.6 6.2 %collective-permute-start = (f32[2,64,128]{2,1,0:T(8,128)S(1)}, f32[2,64,128]{2,1,0:T(8,128)S(1)}, u32[]{:S(2)}, u32[]{:S(2)}) collective-permute-start(f32[2,64,128]{2,1,0:T(8,128)S(1)} %get-tuple-element.24), channel_id=1, source_target_pairs={{0,128},{128,256},{256,384},{1,129},{129,257},{257,385},{2,130},{1... | collective-permute-start | bytes 196616 | tf_op jit(solution)/shard_map/ppermute | solution.py:12
  2.9 6.4 %collective-permute-start.1 = (f32[2,64,128]{2,1,0:T(8,128)S(1)}, f32[2,64,128]{2,1,0:T(8,128)S(1)}, u32[]{:S(2)}, u32[]{:S(2)}) collective-permute-start(f32[2,64,128]{2,1,0:T(8,128)S(1)} %get-tuple-element.23), channel_id=1, source_target_pairs={{128,0},{256,128},{384,256},{129,1},{257,129},{385,257},{130,2},{2... | collective-permute-start | bytes 196616 | tf_op jit(solution)/shard_map/ppermute | solution.py:12
  9.3 1.3 %copy-start.2 = (f32[3,3,128,256]{3,2,1,0:T(8,128)S(1)}, f32[3,3,128,256]{3,2,1,0:T(8,128)}, u32[]{:S(2)}) copy-start(f32[3,3,128,256]{3,2,1,0:T(8,128)} %param.5) | copy-start | bytes 3538948
  9.6 1.8 %copy-start.1 = (f32[8,64,128]{2,1,0:T(8,128)S(1)}, f32[8,64,128]{2,1,0:T(8,128)}, u32[]{:S(2)}) copy-start(f32[8,64,128]{2,1,0:T(8,128)} %param.4) | copy-start | bytes 786436
  15.3 28.7 %all-to-all-start = ((f32[16,40,256]{2,1,0:T(8,128)}), f32[16,40,256]{2,1,0:T(8,128)S(1)}, u32[]{:S(2)}, u32[]{:S(2)}) async-start(f32[16,40,256]{2,1,0:T(8,128)} %bitcast.18), calls=%async_computation | async-start | bytes 1310720 | tf_op jit(solution)/shard_map/all_to_all | solution.py:46
  67.5 12.5 %copy-start.3 = (f32[3,3,256,128]{3,2,1,0:T(8,128)S(1)}, f32[3,3,256,128]{3,2,1,0:T(8,128)}, u32[]{:S(2)}) copy-start(f32[3,3,256,128]{3,2,1,0:T(8,128)} %param.6) | copy-start | bytes 3538948
  68.2 23.1 %collective-permute-start.4 = (f32[9,64,128]{2,1,0:T(8,128)S(1)}, f32[9,64,128]{2,1,0:T(8,128)S(1)}, u32[]{:S(2)}, u32[]{:S(2)}) collective-permute-start(f32[9,64,128]{2,1,0:T(8,128)S(1)} %get-tuple-element.3), channel_id=1, source_target_pairs={{0,384},{128,0},{256,128},{384,256},{1,385},{129,1},{257,129},{385... | collective-permute-start | bytes 884744 | tf_op jit(solution)/shard_map/ppermute | solution.py:12
  72.5 18.8 %collective-permute-start.3 = (f32[9,64,128]{2,1,0:T(8,128)S(1)}, f32[9,64,128]{2,1,0:T(8,128)S(1)}, u32[]{:S(2)}, u32[]{:S(2)}) collective-permute-start(f32[9,64,128]{2,1,0:T(8,128)S(1)} %get-tuple-element.4), channel_id=1, source_target_pairs={{0,256},{128,384},{256,0},{384,128},{1,257},{129,385},{257,1},{385... | collective-permute-start | bytes 884744 | tf_op jit(solution)/shard_map/ppermute | solution.py:12
  75.8 15.5 %collective-permute-start.2 = (f32[9,64,128]{2,1,0:T(8,128)S(1)}, f32[9,64,128]{2,1,0:T(8,128)S(1)}, u32[]{:S(2)}, u32[]{:S(2)}) collective-permute-start(f32[9,64,128]{2,1,0:T(8,128)S(1)} %get-tuple-element.2), channel_id=1, source_target_pairs={{0,128},{128,256},{256,384},{384,0},{1,129},{129,257},{257,385},{3... | collective-permute-start | bytes 884744 | tf_op jit(solution)/shard_map/ppermute | solution.py:12
  84.2 18.7 %all-to-all-start.1 = ((f32[8,8,8,128]{3,2,1,0:T(8,128)}), f32[8,8,8,128]{3,2,1,0:T(8,128)S(1)}, u32[]{:S(2)}, u32[]{:S(2)}) async-start(f32[8,8,8,128]{3,2,1,0:T(8,128)} %bitcast.153), calls=%async_computation.1 | async-start | bytes 524288 | tf_op jit(solution)/shard_map/all_to_all | solution.py:84

commit v2 on v1

v2 whole, which is shorter than its diff:
```python
import functools

import jax
import jax.numpy as jnp
from jax import lax
from jax.experimental import pallas as pl
from jax.experimental.pallas import tpu as pltpu
from jax.sharding import PartitionSpec as P


F32, BF16 = jnp.float32, jnp.bfloat16
VMEM = pl.BlockSpec(memory_space=pltpu.VMEM)
ANY = pl.BlockSpec(memory_space=pl.ANY)
SMEM = pl.BlockSpec(memory_space=pltpu.SMEM)
CORES = 2
LIMIT = pltpu.CompilerParams(vmem_limit_bytes=24 * 2**20)


def near(value):
    return pltpu.with_memory_space_constraint(value, pltpu.VMEM)


def shift(value, axis, step):
    count = lax.axis_size(axis)
    pairs = [(i, i + step) for i in range(count) if 0 <= i + step < count]
    return lax.ppermute(value, axis, pairs)


def turn(value, axis, step):
    count = lax.axis_size(axis)
    return lax.ppermute(value, axis, [(i, (i + step) % count) for i in range(count)])


def split(value):
    high = value.astype(BF16)
    return high, (value - high.astype(F32)).astype(BF16)


def dot(left, right):
    return jnp.dot(left, right, preferred_element_type=F32)


def taps_of_row(row):
    count = row.shape[0]
    at = lax.broadcasted_iota(jnp.int32, row.shape, 0)
    left = jnp.where(at == 0, 0.0, pltpu.roll(row, 1, 0))
    right = jnp.where(at == count - 1, 0.0, pltpu.roll(row, count - 1, 0))
    return left, row, right


def store_taps(row, high, low, start):
    rows, width = row.shape
    for tap, value in enumerate(taps_of_row(row)):
        top, rest = split(value)
        high[start : start + rows, tap * width : (tap + 1) * width] = top
        low[start : start + rows, tap * width : (tap + 1) * width] = rest


def first_prepare(image, weight, high, low, w_high, w_low, image_at, weight_at, sems):
    fetch_image = pltpu.make_async_copy(image, image_at, sems.at[0])
    fetch_weight = pltpu.make_async_copy(weight, weight_at, sems.at[1])
    fetch_image.start()
    fetch_weight.start()
    fetch_image.wait()
    rows, cols, depth = image_at.shape
    for row in range(rows):
        store_taps(image_at[row], high, low, row * cols)
    fetch_weight.wait()
    for tap in range(9):
        top, rest = split(weight_at[tap])
        w_high[tap // 3, (tap % 3) * depth : (tap % 3 + 1) * depth, :] = top
        w_low[tap // 3, (tap % 3) * depth : (tap % 3 + 1) * depth, :] = rest


def half_conv(out, part, cols, high, low, w_high, w_low):
    half = out.shape[0]
    total = None
    for a in range(3):
        rows = pl.ds(pl.multiple_of(part * half + a * cols, cols), half)
        term = dot(high[rows, :], w_high[a])
        term += dot(low[rows, :], w_high[a])
        term += dot(high[rows, :], w_low[a])
        total = term if total is None else total + term
    out[...] = total


def first_given(core, above, below, high_in, low_in, w_high, w_low, given, high, low):
    edge, cols, _ = above.shape
    inner = high_in.shape[0]
    high[edge * cols : edge * cols + inner, :] = high_in[...]
    low[edge * cols : edge * cols + inner, :] = low_in[...]
    for row in range(edge):
        store_taps(above[row], high, low, row * cols)
        store_taps(below[row], high, low, (edge + row) * cols + inner)
    half_conv(given, 1 - core[0], cols, high, low, w_high, w_low)


def first_held(cols, core, high, low, w_high, w_low, held):
    half_conv(held, core[0], cols, high, low, w_high, w_low)


def prepare(weight, grad, w_pair, grad_t):
    depth, wide = weight.shape[1], weight.shape[2]
    for tap in range(9):
        top, rest = split(weight[tap])
        w_pair[tap // 3, (tap % 3) * depth : (tap % 3 + 1) * depth, :wide] = top
        w_pair[tap // 3, (tap % 3) * depth : (tap % 3 + 1) * depth, wide:] = rest
    top, rest = split(grad[...].T)
    grad_t[:wide, :] = top
    grad_t[wide:, :] = rest


def second_conv(slab, hidden, w_from, grad_from, conv, *rest):
    *local, ordered, high, low, turned, w_pair, grad_t, sems = rest
    fetch_grad = pltpu.make_async_copy(grad_from, grad_t, sems.at[0])
    fetch_w = pltpu.make_async_copy(w_from, w_pair, sems.at[1])
    fetch_grad.start()
    fetch_w.start()
    n_in, chunk, depth = hidden.shape
    chips = n_in // CORES
    n_out, rows, width, wide = conv.shape
    cols = n_out * width
    for core in range(CORES):
        for chip in range(chips):
            start = (core * chips + chip) * chunk
            ordered[start : start + chunk, :] = hidden[chip * CORES + core]
    for row in range(rows + 2):
        store_taps(ordered[row * cols : (row + 1) * cols, :], high, low, row * cols)
    slabs = len(local)
    part = local[0].shape[1]
    mine = slab[0]
    pixels = rows * cols
    fetch_grad.wait()
    for a in range(3):
        window = slice(a * cols, a * cols + pixels)
        for b in range(3):
            lanes = slice(b * depth, (b + 1) * depth)
            both = dot(grad_t[...], high[window, lanes])
            total = both[:wide] + both[wide:] + dot(grad_t[:wide, :], low[window, lanes])
            turned[...] = total.T
            for step in range(slabs):
                start = pl.multiple_of(lax.rem(mine + step, slabs) * part, part)
                local[step][a * 3 + b] = turned[pl.ds(start, part), :]
    fetch_w.wait()
    main = None
    other = None
    for a in range(3):
        window = slice(a * cols, a * cols + pixels)
        one = dot(high[window, :], w_pair[a])
        two = dot(low[window, :], w_pair[a, :, :wide])
        main = one if main is None else main + one
        other = two if other is None else other + two
    total = main[:, :wide] + main[:, wide:] + other
    for row in range(rows):
        for block in range(n_out):
            start = row * cols + block * width
            conv[block, row] = total[start : start + width, :]


def block(image_in, first_weight, second_weight, out_grad):
    rows, cols, depth = image_in.shape
    mid = first_weight.shape[3]
    wide = second_weight.shape[3]
    slabs, n_in, n_out = lax.axis_size("slab"), lax.axis_size("cin"), lax.axis_size("cout")
    slab, at = lax.axis_index("slab"), lax.axis_index("cin")
    chips = n_in // CORES
    core = lax.rem(at, CORES)
    ext = (rows + 2) * cols
    half = ext // CORES
    chunk = ext // n_in

    above = shift(image_in[rows - 2 :], "slab", 1)
    below = shift(image_in[:2], "slab", -1)
    weights = [pltpu.VMEM((3, 3 * depth, mid), BF16)] * 2
    inner = [pltpu.VMEM((rows * cols, 3 * depth), BF16)] * 2
    outer = [pltpu.VMEM(((rows + 4) * cols, 3 * depth), BF16)] * 2
    *image_parts, w_high, w_low = pl.pallas_call(
        first_prepare,
        out_shape=inner + weights,
        in_specs=[ANY] * 2,
        out_specs=[VMEM] * 4,
        scratch_shapes=[
            pltpu.VMEM((rows, cols, depth), F32),
            pltpu.VMEM((9, depth, mid), F32),
            pltpu.SemaphoreType.DMA((2,)),
        ],
        name="first_prepare",
        compiler_params=LIMIT,
    )(image_in, first_weight.reshape(9, depth, mid))
    given, high, low = pl.pallas_call(
        first_given,
        out_shape=[pltpu.VMEM((half, mid), F32)] + outer,
        in_specs=[SMEM] + [VMEM] * 6,
        out_specs=[VMEM] * 3,
        name="first_given",
        compiler_params=LIMIT,
    )(core[None], *map(near, (above, below, *image_parts, w_high, w_low)))
    held = pl.pallas_call(
        functools.partial(first_held, cols),
        out_shape=pltpu.VMEM((half, mid), F32),
        in_specs=[SMEM] + [VMEM] * 4,
        out_specs=VMEM,
        name="first_held",
        compiler_params=LIMIT,
    )(core[None], *map(near, (high, low, w_high, w_low)))

    w_pair, grad_t = pl.pallas_call(
        prepare,
        out_shape=[
            jax.ShapeDtypeStruct((3, 3 * mid, 2 * wide), BF16),
            jax.ShapeDtypeStruct((2 * wide, rows * cols), BF16),
        ],
        in_specs=[VMEM] * 2,
        out_specs=[VMEM] * 2,
        name="prepare",
        compiler_params=LIMIT,
    )(second_weight.reshape(9, mid, wide), out_grad.reshape(rows * cols, wide))

    mate = [(i, i ^ 1) for i in range(n_in)]
    held = held + lax.ppermute(given, "cin", mate)
    groups = [[CORES * z + c for z in range(chips)] for c in range(CORES)]
    pieces = lax.all_to_all(
        held.reshape(chips, chunk, mid), "cin", 0, 0, tiled=True, axis_index_groups=groups
    )
    pixel = (core * chips + at // CORES) * chunk + jnp.arange(chunk)
    row_at = slab * rows - 1 + pixel // cols
    inside = (row_at >= 0) & (row_at < slabs * rows)
    own = jnp.where(inside[:, None], jax.nn.silu(jnp.sum(pieces, axis=0)), 0.0)
    hidden = lax.all_gather(own, "cin", axis=0, tiled=False)

    conv, kept, *sent = pl.pallas_call(
        second_conv,
        out_shape=[pltpu.VMEM((n_out, rows, cols // n_out, wide), F32)]
        + [pltpu.VMEM((9, mid // slabs, wide), F32)] * slabs,
        in_specs=[SMEM, VMEM, ANY, ANY],
        out_specs=[VMEM] * (1 + slabs),
        scratch_shapes=[
            pltpu.VMEM((ext, mid), F32),
            pltpu.VMEM((ext, 3 * mid), BF16),
            pltpu.VMEM((ext, 3 * mid), BF16),
            pltpu.VMEM((mid, wide), F32),
            pltpu.VMEM((3, 3 * mid, 2 * wide), BF16),
            pltpu.VMEM((2 * wide, rows * cols), BF16),
            pltpu.SemaphoreType.DMA((2,)),
        ],
        name="second_conv",
        compiler_params=LIMIT,
    )(slab[None], near(hidden), w_pair, grad_t)

    got = {step: turn(sent[step - 1], "slab", step) for step in (2, 1, 3)}
    weight_grad = (kept + got[2] + got[1] + got[3]).reshape(3, 3, mid // slabs, wide)
    gathered = lax.all_to_all(conv, "cout", 0, 0, tiled=True)
    output = jnp.sum(gathered, axis=0)
    return (output, weight_grad)


def solution(mesh):
    in_specs = (
        P("slab", None, "cin"),
        P(None, None, "cin", "cout"),
        P(None, None, "cout", "cin"),
        P("slab", None, "cin"),
    )
    out_specs = (P("slab", "cout", "cin"), P(None, None, ("cout", "slab"), "cin"))
    return jax.shard_map(
        block, mesh=mesh, in_specs=in_specs, out_specs=out_specs, check_vma=False
    )
```

time: 104 us -> 91.7 us (0.88)
  the two profiles are of different devices: /device:TPU:6 before, /device:TPU:64 now
where the time goes in v2:
time: 91.7 us; the launch traced here: 91.2 us
  starting transfers between devices  35.4 us (39%)
  waiting for transfers between devices  25.2 us (27%)
  blocking collectives  17.4 us (19%)
  Pallas kernels  7.05 us (8%)
  local copies, waits for them, and re-layouts  3.11 us (3%)
  other arithmetic  2.28 us (2%)
    all_gather x1, blocking collectives, block(): hidden = lax.all_gather(own, 'cin', axis=0, tiled=False)  17.4 us
    all_to_all x1, waiting for transfers between devices, block(): lax.all_to_all(held.reshape(chips, chunk, mid), 'cin', 0, 0, tiled=True,...  11.8 us
    ppermute x3, starting transfers between devices, turn(): lax.ppermute(value, axis, [(i, (i + step) % count) for i in range(count)])  11.7 us
    all_to_all x1, waiting for transfers between devices, block(): gathered = lax.all_to_all(conv, 'cout', 0, 0, tiled=True)  10.6 us
    all_to_all x1, starting transfers between devices, block(): lax.all_to_all(held.reshape(chips, chunk, mid), 'cin', 0, 0, tiled=True,...  9.96 us
    all_to_all x1, starting transfers between devices, block(): gathered = lax.all_to_all(conv, 'cout', 0, 0, tiled=True)  7.12 us
    ppermute x2, starting transfers between devices, shift(): return lax.ppermute(value, axis, pairs)  4.69 us
    pallas_call x1, Pallas kernels, block(): pl.pallas_call(second_conv, out_shape=[pltpu.VMEM((n_out, rows, cols // n...  4.21 us
  transfers between devices with their start and end apart: 8, of which 5 were waited for; matrix products, arithmetic and copies ran while one was open for 1% of the time, Pallas kernels for 2%

profile of v2, /device:TPU:64, one launch (start us, length us, event | category | flops | bytes accessed | tf_op | source)
XLA Modules:
  0.0 91.2 jit_solution(2681997409750609071)
XLA Ops:
  0.6 0.9 fusion.4
  1.5 3.4 %collective-permute-start = (f32[2,64,128]{2,1,0:T(8,128)S(1)}, f32[2,64,128]{2,1,0:T(8,128)S(1)}, u32[]{:S(2)}, u32[]{:S(2)}) collective-permute-start(f32[2,64,128]{2,1,0:T(8,128)S(1)} %get-tuple-element.31), channel_id=1, source_target_pairs={{0,128},{128,256},{256,384},{1,129},{129,257},{257,385},{2,130},{1... | collective-permute-start | bytes 196616 | tf_op jit(solution)/shard_map/ppermute | solution.py:26
  4.9 1.3 %collective-permute-start.1 = (f32[2,64,128]{2,1,0:T(8,128)S(1)}, f32[2,64,128]{2,1,0:T(8,128)S(1)}, u32[]{:S(2)}, u32[]{:S(2)}) collective-permute-start(f32[2,64,128]{2,1,0:T(8,128)S(1)} %get-tuple-element.30), channel_id=1, source_target_pairs={{128,0},{256,128},{384,256},{129,1},{257,129},{385,257},{130,2},{2... | collective-permute-start | bytes 196616 | tf_op jit(solution)/shard_map/ppermute | solution.py:26
  6.2 1.3 %copy-done = f32[3,3,128,256]{3,2,1,0:T(8,128)S(1)} copy-done((f32[3,3,128,256]{3,2,1,0:T(8,128)S(1)}, f32[3,3,128,256]{3,2,1,0:T(8,128)}, u32[]{:S(2)}) %copy-start) | copy-done | bytes 1179672
  7.5 0.9 %copy-done.2 = f32[8,64,128]{2,1,0:T(8,128)S(1)} copy-done((f32[8,64,128]{2,1,0:T(8,128)S(1)}, f32[8,64,128]{2,1,0:T(8,128)}, u32[]{:S(2)}) %copy-start.2) | copy-done | bytes 262168
  8.5 0.6 first_prepare.1
  9.0 2.0 %collective-permute-done.1.below = f32[2,64,128]{2,1,0:T(8,128)S(1)} collective-permute-done((f32[2,64,128]{2,1,0:T(8,128)S(1)}, f32[2,64,128]{2,1,0:T(8,128)S(1)}, u32[]{:S(2)}, u32[]{:S(2)}) %collective-permute-start.1) | collective-permute-done | bytes 65568 | tf_op jit(solution)/shard_map/ppermute | solution.py:26
  11.1 1.0 %first_given.1 = (f32[320,256]{1,0:T(8,128)S(1)}, bf16[768,384]{1,0:T(8,128)(2,1)S(1)}, bf16[768,384]{1,0:T(8,128)(2,1)S(1)}) custom-call(s32[1]{0:T(128)} %bitcast.1.core, f32[2,64,128]{2,1,0:T(8,128)S(1)} %collective-permute-done.above, f32[2,64,128]{2,1,0:T(8,128)S(1)} %collective-permute-done.1.below, bf16[512,384]{1,0:T(8,128)(2,1)S(1)} %get-tuple-element.16.high_in, ...), custom_call_target="tpu_custom_call" | custom-call | tf_op jit(solution)/shard_map/first_given/pallas_call | solution.py:190
  12.1 1.9 %collective-permute-start.2 = (f32[320,256]{1,0:T(8,128)S(1)}, f32[320,256]{1,0:T(8,128)S(1)}, u32[]{:S(2)}, u32[]{:S(2)}) collective-permute-start(f32[320,256]{1,0:T(8,128)S(1)} %get-tuple-element.22), channel_id=1, source_target_pairs={{0,1},{1,0},{2,3},{3,2},{4,5},{5,4},{6,7},{7,6},{8,9},{9,8},{10,11... | collective-permute-start | bytes 983048 | tf_op jit(solution)/shard_map/ppermute | solution.py:220
  14.0 0.9 %first_held.1 = f32[320,256]{1,0:T(8,128)S(1)} custom-call(s32[1]{0:T(128)} %bitcast.1.core, bf16[768,384]{1,0:T(8,128)(2,1)S(1)} %get-tuple-element.20.high, bf16[768,384]{1,0:T(8,128)(2,1)S(1)} %get-tuple-element.21.low, bf16[3,384,256]{2,1,0:T(8,128)(2,1)S(1)} %get-tuple-element.18.w_high, bf16[3,384,256]{2,1,0:T(8,128)(2,1)S(1)} %get-tuple-element.19.w_low), custom_call_target="tpu_custom_call" | custom-call | tf_op jit(solution)/shard_map/first_held/pallas_call | solution.py:198
  15.0 0.7 collective-permute-done.2
  15.6 0.8 add.58
  16.4 10.0 %all-to-all-start = ((f32[8,40,256]{2,1,0:T(8,128)}), f32[8,40,256]{2,1,0:T(8,128)S(1)}, u32[]{:S(2)}, u32[]{:S(2)}) async-start(f32[8,40,256]{2,1,0:T(8,128)} %bitcast.3), calls=%async_computation | async-start | bytes 655360 | tf_op jit(solution)/shard_map/all_to_all | solution.py:222
  26.4 0.3 prepare.1
  26.7 11.8 %all-to-all-done = f32[8,40,256]{2,1,0:T(8,128)S(1)} async-done(((f32[8,40,256]{2,1,0:T(8,128)}), f32[8,40,256]{2,1,0:T(8,128)S(1)}, u32[]{:S(2)}, u32[]{:S(2)}) %all-to-all-start) | async-done | bytes 327712 | tf_op jit(solution)/shard_map/all_to_all | solution.py:222
  38.6 17.4 %all_gather.4.hidden = f32[16,40,256]{2,1,0:T(8,128)S(1)} all-gather(f32[1,40,256]{2,1,0:T(8,128)S(1)} %fusion.3), channel_id=1, replica_groups=mesh['slab'=4,'cout'=8,'cin'=16] {'cin'}, dimensions={0}, use_global_device_ids=true | all-gather | bytes 696320 | tf_op jit(solution)/shard_map/all_gather | solution.py:229
  56.0 4.2 %second_conv.1 = (f32[8,8,8,128]{3,2,1,0:T(8,128)}, f32[9,64,128]{2,1,0:T(8,128)S(1)}, f32[9,64,128]{2,1,0:T(8,128)S(1)}, f32[9,64,128]{2,1,0:T(8,128)S(1)}, f32[9,64,128]{2,1,0:T(8,128)S(1)}) custom-call(s32[1]{0:T(128)} %bitcast.slab, f32[16,40,256]{2,1,0:T(8,128)S(1)} %all_gather.4.hidden, bf16[3,768,256]{2,1,0:T(8,128)(2,1)S(1)} %get-tuple-element.23.w_from, ...), custom_call_target="tpu_custom_call" | custom-call | tf_op jit(solution)/shard_map/second_conv/pallas_call | solution.py:231
  60.2 4.6 %collective-permute-start.3 = (f32[9,64,128]{2,1,0:T(8,128)S(1)}, f32[9,64,128]{2,1,0:T(8,128)S(1)}, u32[]{:S(2)}, u32[]{:S(2)}) collective-permute-start(f32[9,64,128]{2,1,0:T(8,128)S(1)} %get-tuple-element.27), channel_id=1, source_target_pairs={{0,256},{128,384},{256,0},{384,128},{1,257},{129,385},{257,1},{385... | collective-permute-start | bytes 884744 | tf_op jit(solution)/shard_map/ppermute | solution.py:31
  64.8 1.9 %collective-permute-start.4 = (f32[9,64,128]{2,1,0:T(8,128)S(1)}, f32[9,64,128]{2,1,0:T(8,128)S(1)}, u32[]{:S(2)}, u32[]{:S(2)}) collective-permute-start(f32[9,64,128]{2,1,0:T(8,128)S(1)} %get-tuple-element.28), channel_id=1, source_target_pairs={{0,128},{128,256},{256,384},{384,0},{1,129},{129,257},{257,385},{3... | collective-permute-start | bytes 884744 | tf_op jit(solution)/shard_map/ppermute | solution.py:31
  66.7 5.1 %collective-permute-start.5 = (f32[9,64,128]{2,1,0:T(8,128)S(1)}, f32[9,64,128]{2,1,0:T(8,128)S(1)}, u32[]{:S(2)}, u32[]{:S(2)}) collective-permute-start(f32[9,64,128]{2,1,0:T(8,128)S(1)} %get-tuple-element.29), channel_id=1, source_target_pairs={{0,384},{128,0},{256,128},{384,256},{1,385},{129,1},{257,129},{385... | collective-permute-start | bytes 884744 | tf_op jit(solution)/shard_map/ppermute | solution.py:31
  71.9 7.1 %all-to-all-start.1 = ((f32[8,8,8,128]{3,2,1,0:T(8,128)}), f32[8,8,8,128]{3,2,1,0:T(8,128)S(1)}, u32[]{:S(2)}, u32[]{:S(2)}) async-start(f32[8,8,8,128]{3,2,1,0:T(8,128)} %get-tuple-element.25), calls=%async_computation.1 | async-start | bytes 524288 | tf_op jit(solution)/shard_map/all_to_all | solution.py:252
  79.2 0.8 add_add_fusion
  79.9 10.6 %all-to-all-done.1 = f32[8,8,8,128]{3,2,1,0:T(8,128)S(1)} async-done(((f32[8,8,8,128]{3,2,1,0:T(8,128)}), f32[8,8,8,128]{3,2,1,0:T(8,128)S(1)}, u32[]{:S(2)}, u32[]{:S(2)}) %all-to-all-start.1) | async-done | bytes 262176 | tf_op jit(solution)/shard_map/all_to_all | solution.py:252
  90.6 0.6 reduce_sum.22
  (13 shorter events, 0.3 us)
Async XLA Ops:
  1.5 7.5 %collective-permute-start = (f32[2,64,128]{2,1,0:T(8,128)S(1)}, f32[2,64,128]{2,1,0:T(8,128)S(1)}, u32[]{:S(2)}, u32[]{:S(2)}) collective-permute-start(f32[2,64,128]{2,1,0:T(8,128)S(1)} %get-tuple-element.31), channel_id=1, source_target_pairs={{0,128},{128,256},{256,384},{1,129},{129,257},{257,385},{2,130},{1... | collective-permute-start | bytes 196616 | tf_op jit(solution)/shard_map/ppermute | solution.py:26
  4.9 6.2 %collective-permute-start.1 = (f32[2,64,128]{2,1,0:T(8,128)S(1)}, f32[2,64,128]{2,1,0:T(8,128)S(1)}, u32[]{:S(2)}, u32[]{:S(2)}) collective-permute-start(f32[2,64,128]{2,1,0:T(8,128)S(1)} %get-tuple-element.30), channel_id=1, source_target_pairs={{128,0},{256,128},{384,256},{129,1},{257,129},{385,257},{130,2},{2... | collective-permute-start | bytes 196616 | tf_op jit(solution)/shard_map/ppermute | solution.py:26
  6.2 1.3 %copy-start = (f32[3,3,128,256]{3,2,1,0:T(8,128)S(1)}, f32[3,3,128,256]{3,2,1,0:T(8,128)}, u32[]{:S(2)}) copy-start(f32[3,3,128,256]{3,2,1,0:T(8,128)} %param.5) | copy-start | bytes 3538948
  7.5 0.9 %copy-start.2 = (f32[8,64,128]{2,1,0:T(8,128)S(1)}, f32[8,64,128]{2,1,0:T(8,128)}, u32[]{:S(2)}) copy-start(f32[8,64,128]{2,1,0:T(8,128)} %image.1) | copy-start | bytes 786436
  12.1 3.5 %collective-permute-start.2 = (f32[320,256]{1,0:T(8,128)S(1)}, f32[320,256]{1,0:T(8,128)S(1)}, u32[]{:S(2)}, u32[]{:S(2)}) collective-permute-start(f32[320,256]{1,0:T(8,128)S(1)} %get-tuple-element.22), channel_id=1, source_target_pairs={{0,1},{1,0},{2,3},{3,2},{4,5},{5,4},{6,7},{7,6},{8,9},{9,8},{10,11... | collective-permute-start | bytes 983048 | tf_op jit(solution)/shard_map/ppermute | solution.py:220
  15.0 11.4 %copy-start.1 = (f32[3,3,256,128]{3,2,1,0:T(8,128)S(1)}, f32[3,3,256,128]{3,2,1,0:T(8,128)}, u32[]{:S(2)}) copy-start(f32[3,3,256,128]{3,2,1,0:T(8,128)} %param.6) | copy-start | bytes 3538948
  15.0 11.4 %copy-start.3 = (f32[8,64,128]{2,1,0:T(8,128)S(1)}, f32[8,64,128]{2,1,0:T(8,128)}, u32[]{:S(2)}) copy-start(f32[8,64,128]{2,1,0:T(8,128)} %param.7) | copy-start | bytes 786436
  16.4 22.1 %all-to-all-start = ((f32[8,40,256]{2,1,0:T(8,128)}), f32[8,40,256]{2,1,0:T(8,128)S(1)}, u32[]{:S(2)}, u32[]{:S(2)}) async-start(f32[8,40,256]{2,1,0:T(8,128)} %bitcast.3), calls=%async_computation | async-start | bytes 655360 | tf_op jit(solution)/shard_map/all_to_all | solution.py:222
  60.2 18.8 %collective-permute-start.3 = (f32[9,64,128]{2,1,0:T(8,128)S(1)}, f32[9,64,128]{2,1,0:T(8,128)S(1)}, u32[]{:S(2)}, u32[]{:S(2)}) collective-permute-start(f32[9,64,128]{2,1,0:T(8,128)S(1)} %get-tuple-element.27), channel_id=1, source_target_pairs={{0,256},{128,384},{256,0},{384,128},{1,257},{129,385},{257,1},{385... | collective-permute-start | bytes 884744 | tf_op jit(solution)/shard_map/ppermute | solution.py:31
  64.8 14.3 %collective-permute-start.4 = (f32[9,64,128]{2,1,0:T(8,128)S(1)}, f32[9,64,128]{2,1,0:T(8,128)S(1)}, u32[]{:S(2)}, u32[]{:S(2)}) collective-permute-start(f32[9,64,128]{2,1,0:T(8,128)S(1)} %get-tuple-element.28), channel_id=1, source_target_pairs={{0,128},{128,256},{256,384},{384,0},{1,129},{129,257},{257,385},{3... | collective-permute-start | bytes 884744 | tf_op jit(solution)/shard_map/ppermute | solution.py:31
  66.7 12.4 %collective-permute-start.5 = (f32[9,64,128]{2,1,0:T(8,128)S(1)}, f32[9,64,128]{2,1,0:T(8,128)S(1)}, u32[]{:S(2)}, u32[]{:S(2)}) collective-permute-start(f32[9,64,128]{2,1,0:T(8,128)S(1)} %get-tuple-element.29), channel_id=1, source_target_pairs={{0,384},{128,0},{256,128},{384,256},{1,385},{129,1},{257,129},{385... | collective-permute-start | bytes 884744 | tf_op jit(solution)/shard_map/ppermute | solution.py:31
  71.9 18.7 %all-to-all-start.1 = ((f32[8,8,8,128]{3,2,1,0:T(8,128)}), f32[8,8,8,128]{3,2,1,0:T(8,128)S(1)}, u32[]{:S(2)}, u32[]{:S(2)}) async-start(f32[8,8,8,128]{3,2,1,0:T(8,128)} %get-tuple-element.25), calls=%async_computation.1 | async-start | bytes 524288 | tf_op jit(solution)/shard_map/all_to_all | solution.py:252

commit v3 on v2

--- a/solution.py
+++ b/solution.py
@@ -5,12 +5,12 @@
 from jax import lax
 from jax.experimental import pallas as pl
 from jax.experimental.pallas import tpu as pltpu
-from jax.sharding import PartitionSpec as P
+from jax.sharding import Mesh, PartitionSpec as P
 
 
 F32, BF16 = jnp.float32, jnp.bfloat16
 VMEM = pl.BlockSpec(memory_space=pltpu.VMEM)
-ANY = pl.BlockSpec(memory_space=pl.ANY)
+HBM = pl.BlockSpec(memory_space=pltpu.HBM)
 SMEM = pl.BlockSpec(memory_space=pltpu.SMEM)
 CORES = 2
 LIMIT = pltpu.CompilerParams(vmem_limit_bytes=24 * 2**20)
@@ -18,6 +18,10 @@
 
 def near(value):
     return pltpu.with_memory_space_constraint(value, pltpu.VMEM)
+
+
+def far(value):
+    return pltpu.with_memory_space_constraint(value, pltpu.HBM)
 
 
 def shift(value, axis, step):
@@ -26,9 +30,9 @@
     return lax.ppermute(value, axis, pairs)
 
 
-def turn(value, axis, step):
+def trade(value, axis, step):
     count = lax.axis_size(axis)
-    return lax.ppermute(value, axis, [(i, (i + step) % count) for i in range(count)])
+    return lax.ppermute(value, axis, [(i, i ^ step) for i in range(count)])
 
 
 def split(value):
@@ -110,12 +114,17 @@
     grad_t[wide:, :] = rest
 
 
-def second_conv(slab, hidden, w_from, grad_from, conv, *rest):
-    *local, ordered, high, low, turned, w_pair, grad_t, sems = rest
-    fetch_grad = pltpu.make_async_copy(grad_from, grad_t, sems.at[0])
-    fetch_w = pltpu.make_async_copy(w_from, w_pair, sems.at[1])
-    fetch_grad.start()
-    fetch_w.start()
+def activate(ends, pieces, own):
+    total = pieces[0]
+    for piece in range(1, pieces.shape[0]):
+        total += pieces[piece]
+    pixel = ends[0] + lax.broadcasted_iota(jnp.int32, total.shape, 0)
+    inside = (pixel >= ends[1]) & (pixel < ends[2])
+    own[...] = jnp.where(inside, total / (1.0 + jnp.exp(-total)), 0.0)
+
+
+def second_conv(slab, hidden, w_pair, grad_t, conv, *rest):
+    *local, ordered, high, low, turned = rest
     n_in, chunk, depth = hidden.shape
     chips = n_in // CORES
     n_out, rows, width, wide = conv.shape
@@ -130,7 +139,6 @@
     part = local[0].shape[1]
     mine = slab[0]
     pixels = rows * cols
-    fetch_grad.wait()
     for a in range(3):
         window = slice(a * cols, a * cols + pixels)
         for b in range(3):
@@ -139,9 +147,8 @@
             total = both[:wide] + both[wide:] + dot(grad_t[:wide, :], low[window, lanes])
             turned[...] = total.T
             for step in range(slabs):
-                start = pl.multiple_of(lax.rem(mine + step, slabs) * part, part)
+                start = pl.multiple_of((mine ^ step) * part, part)
                 local[step][a * 3 + b] = turned[pl.ds(start, part), :]
-    fetch_w.wait()
     main = None
     other = None
     for a in range(3):
@@ -161,13 +168,11 @@
     rows, cols, depth = image_in.shape
     mid = first_weight.shape[3]
     wide = second_weight.shape[3]
-    slabs, n_in, n_out = lax.axis_size("slab"), lax.axis_size("cin"), lax.axis_size("cout")
-    slab, at = lax.axis_index("slab"), lax.axis_index("cin")
-    chips = n_in // CORES
-    core = lax.rem(at, CORES)
+    slabs, chips, n_out = lax.axis_size("slab"), lax.axis_size("chip"), lax.axis_size("cout")
+    slab, chip, core = lax.axis_index("slab"), lax.axis_index("chip"), lax.axis_index("core")
     ext = (rows + 2) * cols
     half = ext // CORES
-    chunk = ext // n_in
+    chunk = half // chips
 
     above = shift(image_in[rows - 2 :], "slab", 1)
     below = shift(image_in[:2], "slab", -1)
@@ -177,7 +182,7 @@
     *image_parts, w_high, w_low = pl.pallas_call(
         first_prepare,
         out_shape=inner + weights,
-        in_specs=[ANY] * 2,
+        in_specs=[HBM] * 2,
         out_specs=[VMEM] * 4,
         scratch_shapes=[
             pltpu.VMEM((rows, cols, depth), F32),
@@ -186,7 +191,7 @@
         ],
         name="first_prepare",
         compiler_params=LIMIT,
-    )(image_in, first_weight.reshape(9, depth, mid))
+    )(far(image_in), far(first_weight.reshape(9, depth, mid)))
     given, high, low = pl.pallas_call(
         first_given,
         out_shape=[pltpu.VMEM((half, mid), F32)] + outer,
@@ -207,8 +212,8 @@
     w_pair, grad_t = pl.pallas_call(
         prepare,
         out_shape=[
-            jax.ShapeDtypeStruct((3, 3 * mid, 2 * wide), BF16),
-            jax.ShapeDtypeStruct((2 * wide, rows * cols), BF16),
+            pltpu.VMEM((3, 3 * mid, 2 * wide), BF16),
+            pltpu.VMEM((2 * wide, rows * cols), BF16),
         ],
         in_specs=[VMEM] * 2,
         out_specs=[VMEM] * 2,
@@ -216,38 +221,37 @@
         compiler_params=LIMIT,
     )(second_weight.reshape(9, mid, wide), out_grad.reshape(rows * cols, wide))
 
-    mate = [(i, i ^ 1) for i in range(n_in)]
-    held = held + lax.ppermute(given, "cin", mate)
-    groups = [[CORES * z + c for z in range(chips)] for c in range(CORES)]
-    pieces = lax.all_to_all(
-        held.reshape(chips, chunk, mid), "cin", 0, 0, tiled=True, axis_index_groups=groups
-    )
-    pixel = (core * chips + at // CORES) * chunk + jnp.arange(chunk)
-    row_at = slab * rows - 1 + pixel // cols
-    inside = (row_at >= 0) & (row_at < slabs * rows)
-    own = jnp.where(inside[:, None], jax.nn.silu(jnp.sum(pieces, axis=0)), 0.0)
-    hidden = lax.all_gather(own, "cin", axis=0, tiled=False)
+    held = held + lax.ppermute(given, "core", [(0, 1), (1, 0)])
+    pieces = lax.all_to_all(held.reshape(chips, chunk, mid), "chip", 0, 0, tiled=True)
+    low_end = jnp.where(slab == 0, cols, 0)
+    high_end = jnp.where(slab == slabs - 1, ext - cols, ext)
+    own = pl.pallas_call(
+        activate,
+        out_shape=pltpu.VMEM((chunk, mid), F32),
+        in_specs=[SMEM, VMEM],
+        out_specs=VMEM,
+        name="activate",
+        compiler_params=LIMIT,
+    )(jnp.stack([(core * chips + chip) * chunk, low_end, high_end]), near(pieces))
+    hidden = lax.all_gather(own, ("chip", "core"), axis=0, tiled=False)
 
     conv, kept, *sent = pl.pallas_call(
         second_conv,
         out_shape=[pltpu.VMEM((n_out, rows, cols // n_out, wide), F32)]
         + [pltpu.VMEM((9, mid // slabs, wide), F32)] * slabs,
-        in_specs=[SMEM, VMEM, ANY, ANY],
+        in_specs=[SMEM] + [VMEM] * 3,
         out_specs=[VMEM] * (1 + slabs),
         scratch_shapes=[
             pltpu.VMEM((ext, mid), F32),
             pltpu.VMEM((ext, 3 * mid), BF16),
             pltpu.VMEM((ext, 3 * mid), BF16),
             pltpu.VMEM((mid, wide), F32),
-            pltpu.VMEM((3, 3 * mid, 2 * wide), BF16),
-            pltpu.VMEM((2 * wide, rows * cols), BF16),
-            pltpu.SemaphoreType.DMA((2,)),
         ],
         name="second_conv",
         compiler_params=LIMIT,
-    )(slab[None], near(hidden), w_pair, grad_t)
-
-    got = {step: turn(sent[step - 1], "slab", step) for step in (2, 1, 3)}
+    )(slab[None], near(hidden), near(w_pair), near(grad_t))
+
+    got = {step: trade(sent[step - 1], "slab", step) for step in (2, 1, 3)}
     weight_grad = (kept + got[2] + got[1] + got[3]).reshape(3, 3, mid // slabs, wide)
     gathered = lax.all_to_all(conv, "cout", 0, 0, tiled=True)
     output = jnp.sum(gathered, axis=0)
@@ -255,13 +259,17 @@
 
 
 def solution(mesh):
+    cin = ("chip", "core")
     in_specs = (
-        P("slab", None, "cin"),
-        P(None, None, "cin", "cout"),
-        P(None, None, "cout", "cin"),
-        P("slab", None, "cin"),
+        P("slab", None, cin),
+        P(None, None, cin, "cout"),
+        P(None, None, "cout", cin),
+        P("slab", None, cin),
     )
-    out_specs = (P("slab", "cout", "cin"), P(None, None, ("cout", "slab"), "cin"))
+    out_specs = (P("slab", "cout", cin), P(None, None, ("cout", "slab"), cin))
+    slabs, n_out, n_in = mesh.devices.shape
+    devices = mesh.devices.reshape(slabs, n_out, n_in // CORES, CORES)
+    split_mesh = Mesh(devices, ("slab", "cout", *cin))
     return jax.shard_map(
-        block, mesh=mesh, in_specs=in_specs, out_specs=out_specs, check_vma=False
+        block, mesh=split_mesh, in_specs=in_specs, out_specs=out_specs, check_vma=False
     )

time: 91.7 us -> 90.1 us (0.983)
  the two profiles are of different devices: /device:TPU:64 before, /device:TPU:6 now
where the time goes in v3:
time: 90.1 us; the launch traced here: 89 us
  starting transfers between devices  35.9 us (40%)
  waiting for transfers between devices  25.2 us (28%)
  blocking collectives  16.5 us (18%)
  Pallas kernels  7.51 us (8%)
  other arithmetic  2.25 us (2%)
    all_gather x1, blocking collectives, block(): hidden = lax.all_gather(own, ('chip', 'core'), axis=0, tiled=False)  16.5 us
    all_to_all x1, waiting for transfers between devices, block(): lax.all_to_all(held.reshape(chips, chunk, mid), 'chip', 0, 0, tiled=True)  13.1 us
    ppermute x3, starting transfers between devices, trade(): return lax.ppermute(value, axis, [(i, i ^ step) for i in range(count)])  10.7 us
    all_to_all x1, starting transfers between devices, block(): lax.all_to_all(held.reshape(chips, chunk, mid), 'chip', 0, 0, tiled=True)  10.3 us
    all_to_all x1, waiting for transfers between devices, block(): gathered = lax.all_to_all(conv, 'cout', 0, 0, tiled=True)  9.57 us
    all_to_all x1, starting transfers between devices, block(): gathered = lax.all_to_all(conv, 'cout', 0, 0, tiled=True)  7.12 us
    ppermute x2, starting transfers between devices, shift(): return lax.ppermute(value, axis, pairs)  5.84 us
    pallas_call x1, Pallas kernels, block(): pl.pallas_call(second_conv, out_shape=[pltpu.VMEM((n_out, rows, cols // n...  3.12 us
  transfers between devices with their start and end apart: 8, of which 6 were waited for; matrix products, arithmetic and copies ran while one was open for 1% of the time, Pallas kernels for 3%

profile of v3, /device:TPU:6, one launch (start us, length us, event | category | flops | bytes accessed | tf_op | source)
XLA Modules:
  0.0 89.0 jit_solution(16019309812405531894)
XLA Ops:
  0.6 0.9 fusion
  1.5 1.3 %collective-permute-start = (f32[2,64,128]{2,1,0:T(8,128)S(1)}, f32[2,64,128]{2,1,0:T(8,128)S(1)}, u32[]{:S(2)}, u32[]{:S(2)}) collective-permute-start(f32[2,64,128]{2,1,0:T(8,128)S(1)} %get-tuple-element.31), channel_id=1, source_target_pairs={{0,128},{128,256},{256,384},{1,129},{129,257},{257,385},{2,130},{1... | collective-permute-start | bytes 196616 | tf_op jit(solution)/shard_map/ppermute | solution.py:30
  2.8 4.5 %collective-permute-start.1 = (f32[2,64,128]{2,1,0:T(8,128)S(1)}, f32[2,64,128]{2,1,0:T(8,128)S(1)}, u32[]{:S(2)}, u32[]{:S(2)}) collective-permute-start(f32[2,64,128]{2,1,0:T(8,128)S(1)} %get-tuple-element.30), channel_id=1, source_target_pairs={{128,0},{256,128},{384,256},{129,1},{257,129},{385,257},{130,2},{2... | collective-permute-start | bytes 196616 | tf_op jit(solution)/shard_map/ppermute | solution.py:30
  7.4 1.5 %first_prepare.1 = (bf16[512,384]{1,0:T(8,128)(2,1)S(1)}, bf16[512,384]{1,0:T(8,128)(2,1)S(1)}, bf16[3,384,256]{2,1,0:T(8,128)(2,1)S(1)}, bf16[3,384,256]{2,1,0:T(8,128)(2,1)S(1)}) custom-call(f32[8,64,128]{2,1,0:T(8,128)} %image.1, f32[9,128,256]{2,1,0:T(8,128)} %bitcast.14), custom_call_target="tpu_custom_call" | custom-call | tf_op jit(solution)/shard_map/first_prepare/pallas_call | solution.py:182
  8.9 0.3 collective-permute-done.1.below
  9.3 1.0 %first_given.1 = (f32[320,256]{1,0:T(8,128)S(1)}, bf16[768,384]{1,0:T(8,128)(2,1)S(1)}, bf16[768,384]{1,0:T(8,128)(2,1)S(1)}) custom-call(s32[1]{0:T(128)} %bitcast.4.core, f32[2,64,128]{2,1,0:T(8,128)S(1)} %collective-permute-done.above, f32[2,64,128]{2,1,0:T(8,128)S(1)} %collective-permute-done.1.below, bf16[512,384]{1,0:T(8,128)(2,1)S(1)} %get-tuple-element.16.high_in, ...), custom_call_target="tpu_custom_call" | custom-call | tf_op jit(solution)/shard_map/first_given/pallas_call | solution.py:195
  10.3 1.9 %collective-permute-start.2 = (f32[320,256]{1,0:T(8,128)S(1)}, f32[320,256]{1,0:T(8,128)S(1)}, u32[]{:S(2)}, u32[]{:S(2)}) collective-permute-start(f32[320,256]{1,0:T(8,128)S(1)} %get-tuple-element.22), channel_id=1, source_target_pairs={{0,1},{1,0},{2,3},{3,2},{4,5},{5,4},{6,7},{7,6},{8,9},{9,8},{10,11... | collective-permute-start | bytes 983048 | tf_op jit(solution)/shard_map/ppermute | solution.py:224
  12.2 0.9 %first_held.1 = f32[320,256]{1,0:T(8,128)S(1)} custom-call(s32[1]{0:T(128)} %bitcast.4.core, bf16[768,384]{1,0:T(8,128)(2,1)S(1)} %get-tuple-element.20.high, bf16[768,384]{1,0:T(8,128)(2,1)S(1)} %get-tuple-element.21.low, bf16[3,384,256]{2,1,0:T(8,128)(2,1)S(1)} %get-tuple-element.18.w_high, bf16[3,384,256]{2,1,0:T(8,128)(2,1)S(1)} %get-tuple-element.19.w_low), custom_call_target="tpu_custom_call" | custom-call | tf_op jit(solution)/shard_map/first_held/pallas_call | solution.py:203
  13.2 0.6 collective-permute-done.2
  13.8 0.8 add.16
  14.6 10.3 %all-to-all-start = ((f32[8,40,256]{2,1,0:T(8,128)}), f32[8,40,256]{2,1,0:T(8,128)S(1)}, u32[]{:S(2)}, u32[]{:S(2)}) async-start(f32[8,40,256]{2,1,0:T(8,128)} %bitcast.6), calls=%async_computation | async-start | bytes 655360 | tf_op jit(solution)/shard_map/all_to_all | solution.py:225
  25.3 13.1 %all-to-all-done.pieces = f32[8,40,256]{2,1,0:T(8,128)S(1)} async-done(((f32[8,40,256]{2,1,0:T(8,128)}), f32[8,40,256]{2,1,0:T(8,128)S(1)}, u32[]{:S(2)}, u32[]{:S(2)}) %all-to-all-start) | async-done | bytes 327712 | tf_op jit(solution)/shard_map/all_to_all | solution.py:225
  38.5 0.6 activate.1
  39.1 16.5 %all-gather = f32[640,256]{1,0:T(8,128)S(1)} all-gather(f32[40,256]{1,0:T(8,128)S(1)} %activate.1), channel_id=2, replica_groups=mesh['slab'=4,'cout'=8,'chip'=8,'core'=2] {'chip','core'}, dimensions={0}, use_global_device_ids=true | all-gather | bytes 696320 | tf_op jit(solution)/shard_map/all_gather | solution.py:236
  55.5 3.1 %second_conv.1 = (f32[8,8,8,128]{3,2,1,0:T(8,128)}, f32[9,64,128]{2,1,0:T(8,128)S(1)}, f32[9,64,128]{2,1,0:T(8,128)S(1)}, f32[9,64,128]{2,1,0:T(8,128)S(1)}, f32[9,64,128]{2,1,0:T(8,128)S(1)}) custom-call(s32[1]{0:T(128)} %bitcast.slab, f32[16,40,256]{2,1,0:T(8,128)S(1)} %bitcast.11, bf16[3,768,256]{2,1,0:T(8,128)(2,1)S(1)} %get-tuple-element.23.w_pair, ...), custom_call_target="tpu_custom_call" | custom-call | tf_op jit(solution)/shard_map/second_conv/pallas_call | solution.py:238
  58.7 5.1 %collective-permute-start.3 = (f32[9,64,128]{2,1,0:T(8,128)S(1)}, f32[9,64,128]{2,1,0:T(8,128)S(1)}, u32[]{:S(2)}, u32[]{:S(2)}) collective-permute-start(f32[9,64,128]{2,1,0:T(8,128)S(1)} %get-tuple-element.27), channel_id=1, source_target_pairs={{0,256},{128,384},{256,0},{384,128},{1,257},{129,385},{257,1},{385... | collective-permute-start | bytes 884744 | tf_op jit(solution)/shard_map/ppermute | solution.py:35
  63.8 1.9 %collective-permute-start.4 = (f32[9,64,128]{2,1,0:T(8,128)S(1)}, f32[9,64,128]{2,1,0:T(8,128)S(1)}, u32[]{:S(2)}, u32[]{:S(2)}) collective-permute-start(f32[9,64,128]{2,1,0:T(8,128)S(1)} %get-tuple-element.28), channel_id=1, source_target_pairs={{0,128},{128,0},{256,384},{384,256},{1,129},{129,1},{257,385},{385... | collective-permute-start | bytes 884744 | tf_op jit(solution)/shard_map/ppermute | solution.py:35
  65.7 3.7 %collective-permute-start.5 = (f32[9,64,128]{2,1,0:T(8,128)S(1)}, f32[9,64,128]{2,1,0:T(8,128)S(1)}, u32[]{:S(2)}, u32[]{:S(2)}) collective-permute-start(f32[9,64,128]{2,1,0:T(8,128)S(1)} %get-tuple-element.29), channel_id=1, source_target_pairs={{0,384},{128,256},{256,128},{384,0},{1,385},{129,257},{257,129},{3... | collective-permute-start | bytes 884744 | tf_op jit(solution)/shard_map/ppermute | solution.py:35
  69.4 7.1 %all-to-all-start.1 = ((f32[8,8,8,128]{3,2,1,0:T(8,128)}), f32[8,8,8,128]{3,2,1,0:T(8,128)S(1)}, u32[]{:S(2)}, u32[]{:S(2)}) async-start(f32[8,8,8,128]{3,2,1,0:T(8,128)} %get-tuple-element.25), calls=%async_computation.1 | async-start | bytes 524288 | tf_op jit(solution)/shard_map/all_to_all | solution.py:256
  76.6 0.7 collective-permute-done.4
  77.3 0.8 collective-permute-done.5
  78.0 0.8 add_add_fusion
  78.8 9.6 %all-to-all-done.1 = f32[8,8,8,128]{3,2,1,0:T(8,128)S(1)} async-done(((f32[8,8,8,128]{3,2,1,0:T(8,128)}), f32[8,8,8,128]{3,2,1,0:T(8,128)S(1)}, u32[]{:S(2)}, u32[]{:S(2)}) %all-to-all-start.1) | async-done | bytes 262176 | tf_op jit(solution)/shard_map/all_to_all | solution.py:256
  88.4 0.6 reduce_sum.9
  (8 shorter events, 0.4 us)
Async XLA Ops:
  1.5 7.4 %collective-permute-start = (f32[2,64,128]{2,1,0:T(8,128)S(1)}, f32[2,64,128]{2,1,0:T(8,128)S(1)}, u32[]{:S(2)}, u32[]{:S(2)}) collective-permute-start(f32[2,64,128]{2,1,0:T(8,128)S(1)} %get-tuple-element.31), channel_id=1, source_target_pairs={{0,128},{128,256},{256,384},{1,129},{129,257},{257,385},{2,130},{1... | collective-permute-start | bytes 196616 | tf_op jit(solution)/shard_map/ppermute | solution.py:30
  2.8 6.4 %collective-permute-start.1 = (f32[2,64,128]{2,1,0:T(8,128)S(1)}, f32[2,64,128]{2,1,0:T(8,128)S(1)}, u32[]{:S(2)}, u32[]{:S(2)}) collective-permute-start(f32[2,64,128]{2,1,0:T(8,128)S(1)} %get-tuple-element.30), channel_id=1, source_target_pairs={{128,0},{256,128},{384,256},{129,1},{257,129},{385,257},{130,2},{2... | collective-permute-start | bytes 196616 | tf_op jit(solution)/shard_map/ppermute | solution.py:30
  10.3 3.5 %collective-permute-start.2 = (f32[320,256]{1,0:T(8,128)S(1)}, f32[320,256]{1,0:T(8,128)S(1)}, u32[]{:S(2)}, u32[]{:S(2)}) collective-permute-start(f32[320,256]{1,0:T(8,128)S(1)} %get-tuple-element.22), channel_id=1, source_target_pairs={{0,1},{1,0},{2,3},{3,2},{4,5},{5,4},{6,7},{7,6},{8,9},{9,8},{10,11... | collective-permute-start | bytes 983048 | tf_op jit(solution)/shard_map/ppermute | solution.py:224
  13.2 11.8 %copy-start = (f32[3,3,256,128]{3,2,1,0:T(8,128)S(1)}, f32[3,3,256,128]{3,2,1,0:T(8,128)}, u32[]{:S(2)}) copy-start(f32[3,3,256,128]{3,2,1,0:T(8,128)} %param.6) | copy-start | bytes 3538948
  13.2 11.7 %copy-start.1 = (f32[8,64,128]{2,1,0:T(8,128)S(1)}, f32[8,64,128]{2,1,0:T(8,128)}, u32[]{:S(2)}) copy-start(f32[8,64,128]{2,1,0:T(8,128)} %param.7) | copy-start | bytes 786436
  14.6 23.9 %all-to-all-start = ((f32[8,40,256]{2,1,0:T(8,128)}), f32[8,40,256]{2,1,0:T(8,128)S(1)}, u32[]{:S(2)}, u32[]{:S(2)}) async-start(f32[8,40,256]{2,1,0:T(8,128)} %bitcast.6), calls=%async_computation | async-start | bytes 655360 | tf_op jit(solution)/shard_map/all_to_all | solution.py:225
  58.7 17.9 %collective-permute-start.3 = (f32[9,64,128]{2,1,0:T(8,128)S(1)}, f32[9,64,128]{2,1,0:T(8,128)S(1)}, u32[]{:S(2)}, u32[]{:S(2)}) collective-permute-start(f32[9,64,128]{2,1,0:T(8,128)S(1)} %get-tuple-element.27), channel_id=1, source_target_pairs={{0,256},{128,384},{256,0},{384,128},{1,257},{129,385},{257,1},{385... | collective-permute-start | bytes 884744 | tf_op jit(solution)/shard_map/ppermute | solution.py:35
  63.8 13.5 %collective-permute-start.4 = (f32[9,64,128]{2,1,0:T(8,128)S(1)}, f32[9,64,128]{2,1,0:T(8,128)S(1)}, u32[]{:S(2)}, u32[]{:S(2)}) collective-permute-start(f32[9,64,128]{2,1,0:T(8,128)S(1)} %get-tuple-element.28), channel_id=1, source_target_pairs={{0,128},{128,0},{256,384},{384,256},{1,129},{129,1},{257,385},{385... | collective-permute-start | bytes 884744 | tf_op jit(solution)/shard_map/ppermute | solution.py:35
  65.7 12.3 %collective-permute-start.5 = (f32[9,64,128]{2,1,0:T(8,128)S(1)}, f32[9,64,128]{2,1,0:T(8,128)S(1)}, u32[]{:S(2)}, u32[]{:S(2)}) collective-permute-start(f32[9,64,128]{2,1,0:T(8,128)S(1)} %get-tuple-element.29), channel_id=1, source_target_pairs={{0,384},{128,256},{256,128},{384,0},{1,385},{129,257},{257,129},{3... | collective-permute-start | bytes 884744 | tf_op jit(solution)/shard_map/ppermute | solution.py:35
  69.4 18.9 %all-to-all-start.1 = ((f32[8,8,8,128]{3,2,1,0:T(8,128)}), f32[8,8,8,128]{3,2,1,0:T(8,128)S(1)}, u32[]{:S(2)}, u32[]{:S(2)}) async-start(f32[8,8,8,128]{3,2,1,0:T(8,128)} %get-tuple-element.25), calls=%async_computation.1 | async-start | bytes 524288 | tf_op jit(solution)/shard_map/all_to_all | solution.py:256

commit v4 on v3

--- a/solution.py
+++ b/solution.py
@@ -103,15 +103,21 @@
     half_conv(held, core[0], cols, high, low, w_high, w_low)
 
 
-def prepare(weight, grad, w_pair, grad_t):
+def prepare(weight, w_pair):
     depth, wide = weight.shape[1], weight.shape[2]
     for tap in range(9):
         top, rest = split(weight[tap])
         w_pair[tap // 3, (tap % 3) * depth : (tap % 3 + 1) * depth, :wide] = top
         w_pair[tap // 3, (tap % 3) * depth : (tap % 3 + 1) * depth, wide:] = rest
-    top, rest = split(grad[...].T)
-    grad_t[:wide, :] = top
-    grad_t[wide:, :] = rest
+
+
+def turn_grads(slab, *refs):
+    *grads, grad_t = refs
+    wide = grads[0].shape[1]
+    for step, grad in enumerate(grads):
+        top, rest = split(grad[...].T)
+        grad_t[slab[0] ^ step, :wide, :] = top
+        grad_t[slab[0] ^ step, wide:, :] = rest
 
 
 def activate(ends, pieces, own):
@@ -123,9 +129,17 @@
     own[...] = jnp.where(inside, total / (1.0 + jnp.exp(-total)), 0.0)
 
 
-def second_conv(slab, hidden, w_pair, grad_t, conv, *rest):
-    *local, ordered, high, low, turned = rest
-    n_in, chunk, depth = hidden.shape
+def lower_lanes(shape):
+    return lax.broadcasted_iota(jnp.int32, shape, 1) < shape[1] // 2
+
+
+def swap_lanes(value):
+    return pltpu.roll(value, value.shape[1] // 2, 1)
+
+
+def second_conv(slab, hidden, w_pair, conv, *rest):
+    *local, ordered, high, low, packed = rest
+    n_in, chunk, _ = hidden.shape
     chips = n_in // CORES
     n_out, rows, width, wide = conv.shape
     cols = n_out * width
@@ -133,22 +147,21 @@
         for chip in range(chips):
             start = (core * chips + chip) * chunk
             ordered[start : start + chunk, :] = hidden[chip * CORES + core]
+    count, lanes = local[0].shape
+    for quarter in range(len(local)):
+        at = slice(quarter // 2 * lanes, (quarter // 2 + 1) * lanes)
+        first = ordered[cols : cols + count, at]
+        second = ordered[cols + count : cols + 2 * count, at]
+        if quarter % 2:
+            first = swap_lanes(first)
+        else:
+            second = swap_lanes(second)
+        packed[quarter] = jnp.where(lower_lanes(first.shape), first, second)
+    for step, out in enumerate(local):
+        out[...] = packed[slab[0] ^ step]
     for row in range(rows + 2):
         store_taps(ordered[row * cols : (row + 1) * cols, :], high, low, row * cols)
-    slabs = len(local)
-    part = local[0].shape[1]
-    mine = slab[0]
     pixels = rows * cols
-    for a in range(3):
-        window = slice(a * cols, a * cols + pixels)
-        for b in range(3):
-            lanes = slice(b * depth, (b + 1) * depth)
-            both = dot(grad_t[...], high[window, lanes])
-            total = both[:wide] + both[wide:] + dot(grad_t[:wide, :], low[window, lanes])
-            turned[...] = total.T
-            for step in range(slabs):
-                start = pl.multiple_of((mine ^ step) * part, part)
-                local[step][a * 3 + b] = turned[pl.ds(start, part), :]
     main = None
     other = None
     for a in range(3):
@@ -162,6 +175,46 @@
         for block in range(n_out):
             start = row * cols + block * width
             conv[block, row] = total[start : start + width, :]
+
+
+def weight_sums(cols, slab, *refs):
+    *local, grad_t, out, high, low = refs
+    slabs = len(local)
+    count, lanes = local[0].shape
+    part = lanes // 2
+    wide = out.shape[2]
+    blank = jnp.zeros((cols, 2 * lanes), BF16)
+    end = high.shape[0] - cols
+    for ref in (high, low):
+        ref[0:cols, :] = blank
+        ref[end : end + cols, :] = blank
+    for step, source in enumerate(local):
+        base = cols + (slab[0] ^ step) * 2 * count
+        for row in range(count // cols):
+            left, here, right = taps_of_row(source[row * cols : (row + 1) * cols, :])
+            lower = lower_lanes(here.shape)
+            pairs = (
+                (jnp.where(lower, left, swap_lanes(here)), right),
+                (jnp.where(lower, swap_lanes(left), here), swap_lanes(right)),
+            )
+            for half, pair in enumerate(pairs):
+                start = pl.multiple_of(base + half * count + row * cols, cols)
+                for k, value in enumerate(pair):
+                    top, rest = split(value)
+                    high[pl.ds(start, cols), k * lanes : (k + 1) * lanes] = top
+                    low[pl.ds(start, cols), k * lanes : (k + 1) * lanes] = rest
+    for a in range(3):
+        main = None
+        other = None
+        for j in range(slabs):
+            window = slice(a * cols + j * 2 * count, a * cols + (j + 1) * 2 * count)
+            one = dot(grad_t[j], high[window, :])
+            two = dot(grad_t[j, :wide, :], low[window, :])
+            main = one if main is None else main + one
+            other = two if other is None else other + two
+        turned = (main[:wide] + main[wide:] + other).T
+        for b in range(3):
+            out[a * 3 + b] = turned[b * part : (b + 1) * part, :]
 
 
 def block(image_in, first_weight, second_weight, out_grad):
@@ -209,20 +262,19 @@
         compiler_params=LIMIT,
     )(core[None], *map(near, (high, low, w_high, w_low)))
 
-    w_pair, grad_t = pl.pallas_call(
+    w_pair = pl.pallas_call(
         prepare,
-        out_shape=[
-            pltpu.VMEM((3, 3 * mid, 2 * wide), BF16),
-            pltpu.VMEM((2 * wide, rows * cols), BF16),
-        ],
-        in_specs=[VMEM] * 2,
-        out_specs=[VMEM] * 2,
+        out_shape=pltpu.VMEM((3, 3 * mid, 2 * wide), BF16),
+        in_specs=[VMEM],
+        out_specs=VMEM,
         name="prepare",
         compiler_params=LIMIT,
-    )(second_weight.reshape(9, mid, wide), out_grad.reshape(rows * cols, wide))
+    )(second_weight.reshape(9, mid, wide))
 
     held = held + lax.ppermute(given, "core", [(0, 1), (1, 0)])
     pieces = lax.all_to_all(held.reshape(chips, chunk, mid), "chip", 0, 0, tiled=True)
+    grads = [out_grad.reshape(rows * cols, wide)]
+    grads += [trade(grads[0], "slab", step) for step in range(1, slabs)]
     low_end = jnp.where(slab == 0, cols, 0)
     high_end = jnp.where(slab == slabs - 1, ext - cols, ext)
     own = pl.pallas_call(
@@ -235,25 +287,47 @@
     )(jnp.stack([(core * chips + chip) * chunk, low_end, high_end]), near(pieces))
     hidden = lax.all_gather(own, ("chip", "core"), axis=0, tiled=False)
 
-    conv, kept, *sent = pl.pallas_call(
+    lanes = 2 * mid // slabs
+    count = rows * cols // 2
+    conv, *local = pl.pallas_call(
         second_conv,
         out_shape=[pltpu.VMEM((n_out, rows, cols // n_out, wide), F32)]
-        + [pltpu.VMEM((9, mid // slabs, wide), F32)] * slabs,
-        in_specs=[SMEM] + [VMEM] * 3,
+        + [pltpu.VMEM((count, lanes), F32)] * slabs,
+        in_specs=[SMEM] + [VMEM] * 2,
         out_specs=[VMEM] * (1 + slabs),
         scratch_shapes=[
             pltpu.VMEM((ext, mid), F32),
             pltpu.VMEM((ext, 3 * mid), BF16),
             pltpu.VMEM((ext, 3 * mid), BF16),
-            pltpu.VMEM((mid, wide), F32),
+            pltpu.VMEM((slabs, count, lanes), F32),
         ],
         name="second_conv",
         compiler_params=LIMIT,
-    )(slab[None], near(hidden), near(w_pair), near(grad_t))
-
-    got = {step: trade(sent[step - 1], "slab", step) for step in (2, 1, 3)}
-    weight_grad = (kept + got[2] + got[1] + got[3]).reshape(3, 3, mid // slabs, wide)
+    )(slab[None], near(hidden), near(w_pair))
+
     gathered = lax.all_to_all(conv, "cout", 0, 0, tiled=True)
+    local[1:] = [trade(local[step], "slab", step) for step in range(1, slabs)]
+    grad_t = pl.pallas_call(
+        turn_grads,
+        out_shape=pltpu.VMEM((slabs, 2 * wide, rows * cols), BF16),
+        in_specs=[SMEM] + [VMEM] * slabs,
+        out_specs=VMEM,
+        name="turn_grads",
+        compiler_params=LIMIT,
+    )(slab[None], *map(near, grads))
+    weight_grad = pl.pallas_call(
+        functools.partial(weight_sums, cols),
+        out_shape=jax.ShapeDtypeStruct((9, mid // slabs, wide), F32),
+        in_specs=[SMEM] + [VMEM] * (slabs + 1),
+        out_specs=VMEM,
+        scratch_shapes=[
+            pltpu.VMEM(((slabs * rows + 2) * cols, 2 * lanes), BF16),
+            pltpu.VMEM(((slabs * rows + 2) * cols, 2 * lanes), BF16),
+        ],
+        name="weight_sums",
+        compiler_params=LIMIT,
+    )(slab[None], *map(near, local), near(grad_t))
+    weight_grad = weight_grad.reshape(3, 3, mid // slabs, wide)
     output = jnp.sum(gathered, axis=0)
     return (output, weight_grad)
 

time: 90.1 us -> 99.6 us (1.11)
  the two profiles are of different devices: /device:TPU:6 before, /device:TPU:1 now
where the time goes in v4:
time: 99.6 us; the launch traced here: 99 us
  starting transfers between devices  45.3 us (45%)
  waiting for transfers between devices  24.2 us (24%)
  blocking collectives  16.9 us (17%)
  Pallas kernels  9.41 us (9%)
  other arithmetic  1.47 us (1%)
    ppermute x6, starting transfers between devices, trade(): return lax.ppermute(value, axis, [(i, i ^ step) for i in range(count)])  19.2 us
    all_gather x1, blocking collectives, block(): hidden = lax.all_gather(own, ('chip', 'core'), axis=0, tiled=False)  16.9 us
    all_to_all x1, waiting for transfers between devices, block(): lax.all_to_all(held.reshape(chips, chunk, mid), 'chip', 0, 0, tiled=True)  13.3 us
    ppermute x6, waiting for transfers between devices, trade(): return lax.ppermute(value, axis, [(i, i ^ step) for i in range(count)])  8.38 us
    ppermute x1, starting transfers between devices, block(): held = held + lax.ppermute(given, 'core', [(0, 1), (1, 0)])  7.25 us
    all_to_all x1, starting transfers between devices, block(): gathered = lax.all_to_all(conv, 'cout', 0, 0, tiled=True)  6.82 us
    all_to_all x1, starting transfers between devices, block(): lax.all_to_all(held.reshape(chips, chunk, mid), 'chip', 0, 0, tiled=True)  6.79 us
    ppermute x2, starting transfers between devices, shift(): return lax.ppermute(value, axis, pairs)  5.23 us
  transfers between devices with their start and end apart: 11, of which 5 were waited for; matrix products, arithmetic and copies ran while one was open for 0% of the time, Pallas kernels for 6%

profile of v4, /device:TPU:1, one launch (start us, length us, event | category | flops | bytes accessed | tf_op | source)
XLA Modules:
  0.0 99.0 jit_solution(12017362969443802759)
XLA Ops:
  0.6 0.9 fusion
  1.5 3.9 %collective-permute-start = (f32[2,64,128]{2,1,0:T(8,128)S(1)}, f32[2,64,128]{2,1,0:T(8,128)S(1)}, u32[]{:S(2)}, u32[]{:S(2)}) collective-permute-start(f32[2,64,128]{2,1,0:T(8,128)S(1)} %get-tuple-element.27), channel_id=1, source_target_pairs={{0,128},{128,256},{256,384},{1,129},{129,257},{257,385},{2,130},{1... | collective-permute-start | bytes 196616 | tf_op jit(solution)/shard_map/ppermute | solution.py:30
  5.5 1.3 %collective-permute-start.1 = (f32[2,64,128]{2,1,0:T(8,128)S(1)}, f32[2,64,128]{2,1,0:T(8,128)S(1)}, u32[]{:S(2)}, u32[]{:S(2)}) collective-permute-start(f32[2,64,128]{2,1,0:T(8,128)S(1)} %get-tuple-element.26), channel_id=1, source_target_pairs={{128,0},{256,128},{384,256},{129,1},{257,129},{385,257},{130,2},{2... | collective-permute-start | bytes 196616 | tf_op jit(solution)/shard_map/ppermute | solution.py:30
  6.8 1.5 %first_prepare.1 = (bf16[512,384]{1,0:T(8,128)(2,1)S(1)}, bf16[512,384]{1,0:T(8,128)(2,1)S(1)}, bf16[3,384,256]{2,1,0:T(8,128)(2,1)S(1)}, bf16[3,384,256]{2,1,0:T(8,128)(2,1)S(1)}) custom-call(f32[8,64,128]{2,1,0:T(8,128)} %image.1, f32[9,128,256]{2,1,0:T(8,128)} %bitcast.17), custom_call_target="tpu_custom_call" | custom-call | tf_op jit(solution)/shard_map/first_prepare/pallas_call | solution.py:235
  8.3 2.2 %collective-permute-done.1.below = f32[2,64,128]{2,1,0:T(8,128)S(1)} collective-permute-done((f32[2,64,128]{2,1,0:T(8,128)S(1)}, f32[2,64,128]{2,1,0:T(8,128)S(1)}, u32[]{:S(2)}, u32[]{:S(2)}) %collective-permute-start.1) | collective-permute-done | bytes 65568 | tf_op jit(solution)/shard_map/ppermute | solution.py:30
  10.5 1.0 %first_given.1 = (f32[320,256]{1,0:T(8,128)S(1)}, bf16[768,384]{1,0:T(8,128)(2,1)S(1)}, bf16[768,384]{1,0:T(8,128)(2,1)S(1)}) custom-call(s32[1]{0:T(128)} %bitcast.4.core, f32[2,64,128]{2,1,0:T(8,128)S(1)} %collective-permute-done.above, f32[2,64,128]{2,1,0:T(8,128)S(1)} %collective-permute-done.1.below, bf16[512,384]{1,0:T(8,128)(2,1)S(1)} %get-tuple-element.14.high_in, ...), custom_call_target="tpu_custom_call" | custom-call | tf_op jit(solution)/shard_map/first_given/pallas_call | solution.py:248
  11.5 7.3 %collective-permute-start.2 = (f32[320,256]{1,0:T(8,128)S(1)}, f32[320,256]{1,0:T(8,128)S(1)}, u32[]{:S(2)}, u32[]{:S(2)}) collective-permute-start(f32[320,256]{1,0:T(8,128)S(1)} %get-tuple-element.20), channel_id=1, source_target_pairs={{0,1},{1,0},{2,3},{3,2},{4,5},{5,4},{6,7},{7,6},{8,9},{9,8},{10,11... | collective-permute-start | bytes 983048 | tf_op jit(solution)/shard_map/ppermute | solution.py:274
  18.8 0.9 first_held.1
  20.0 0.8 add.7
  20.8 6.8 %all-to-all-start = ((f32[8,40,256]{2,1,0:T(8,128)}), f32[8,40,256]{2,1,0:T(8,128)S(1)}, u32[]{:S(2)}, u32[]{:S(2)}) async-start(f32[8,40,256]{2,1,0:T(8,128)} %bitcast.6), calls=%async_computation | async-start | bytes 655360 | tf_op jit(solution)/shard_map/all_to_all | solution.py:275
  27.9 13.3 %all-to-all-done.pieces = f32[8,40,256]{2,1,0:T(8,128)S(1)} async-done(((f32[8,40,256]{2,1,0:T(8,128)}), f32[8,40,256]{2,1,0:T(8,128)S(1)}, u32[]{:S(2)}, u32[]{:S(2)}) %all-to-all-start) | async-done | bytes 327712 | tf_op jit(solution)/shard_map/all_to_all | solution.py:275
  41.8 16.9 %all-gather = f32[640,256]{1,0:T(8,128)S(1)} all-gather(f32[40,256]{1,0:T(8,128)S(1)} %activate.1), channel_id=2, replica_groups=mesh['slab'=4,'cout'=8,'chip'=8,'core'=2] {'chip','core'}, dimensions={0}, use_global_device_ids=true | all-gather | bytes 696320 | tf_op jit(solution)/shard_map/all_gather | solution.py:288
  58.7 2.1 %second_conv.1 = (f32[8,8,8,128]{3,2,1,0:T(8,128)}, f32[256,128]{1,0:T(8,128)S(1)}, f32[256,128]{1,0:T(8,128)S(1)}, f32[256,128]{1,0:T(8,128)S(1)}, f32[256,128]{1,0:T(8,128)S(1)}) custom-call(s32[1]{0:T(128)} %bitcast.slab, f32[16,40,256]{2,1,0:T(8,128)S(1)} %bitcast.11, bf16[3,768,256]{2,1,0:T(8,128)(2,1)S(1)} %prepare.1.w_pair), custom_call_target="tpu_custom_call" | custom-call | tf_op jit(solution)/shard_map/second_conv/pallas_call | solution.py:292
  60.8 6.8 %all-to-all-start.1 = ((f32[8,8,8,128]{3,2,1,0:T(8,128)}), f32[8,8,8,128]{3,2,1,0:T(8,128)S(1)}, u32[]{:S(2)}, u32[]{:S(2)}) async-start(f32[8,8,8,128]{3,2,1,0:T(8,128)} %get-tuple-element.21), calls=%async_computation.1 | async-start | bytes 524288 | tf_op jit(solution)/shard_map/all_to_all | solution.py:308
  67.7 3.1 %collective-permute-start.6 = (f32[512,128]{1,0:T(8,128)S(1)}, f32[512,128]{1,0:T(8,128)S(1)}, u32[]{:S(2)}, u32[]{:S(2)}) collective-permute-start(f32[512,128]{1,0:T(8,128)S(1)} %bitcast.13), channel_id=1, source_target_pairs={{0,128},{128,0},{256,384},{384,256},{1,129},{129,1},{257,385},{385... | collective-permute-start | bytes 786440 | tf_op jit(solution)/shard_map/ppermute | solution.py:35
  70.8 3.2 %collective-permute-start.7 = (f32[512,128]{1,0:T(8,128)S(1)}, f32[512,128]{1,0:T(8,128)S(1)}, u32[]{:S(2)}, u32[]{:S(2)}) collective-permute-start(f32[512,128]{1,0:T(8,128)S(1)} %bitcast.14), channel_id=1, source_target_pairs={{0,256},{128,384},{256,0},{384,128},{1,257},{129,385},{257,1},{385... | collective-permute-start | bytes 786440 | tf_op jit(solution)/shard_map/ppermute | solution.py:35
  74.0 3.3 %collective-permute-start.8 = (f32[512,128]{1,0:T(8,128)S(1)}, f32[512,128]{1,0:T(8,128)S(1)}, u32[]{:S(2)}, u32[]{:S(2)}) collective-permute-start(f32[512,128]{1,0:T(8,128)S(1)} %bitcast.15), channel_id=1, source_target_pairs={{0,384},{128,256},{256,128},{384,0},{1,385},{129,257},{257,129},{3... | collective-permute-start | bytes 786440 | tf_op jit(solution)/shard_map/ppermute | solution.py:35
  77.3 1.9 %collective-permute-start.3 = (f32[256,128]{1,0:T(8,128)S(1)}, f32[256,128]{1,0:T(8,128)S(1)}, u32[]{:S(2)}, u32[]{:S(2)}) collective-permute-start(f32[256,128]{1,0:T(8,128)S(1)} %get-tuple-element.23), channel_id=1, source_target_pairs={{0,128},{128,0},{256,384},{384,256},{1,129},{129,1},{257,385},{385... | collective-permute-start | bytes 393224 | tf_op jit(solution)/shard_map/ppermute | solution.py:35
  79.2 4.4 %collective-permute-start.4 = (f32[256,128]{1,0:T(8,128)S(1)}, f32[256,128]{1,0:T(8,128)S(1)}, u32[]{:S(2)}, u32[]{:S(2)}) collective-permute-start(f32[256,128]{1,0:T(8,128)S(1)} %get-tuple-element.24), channel_id=1, source_target_pairs={{0,256},{128,384},{256,0},{384,128},{1,257},{129,385},{257,1},{385... | collective-permute-start | bytes 393224 | tf_op jit(solution)/shard_map/ppermute | solution.py:35
  83.6 3.3 %collective-permute-start.5 = (f32[256,128]{1,0:T(8,128)S(1)}, f32[256,128]{1,0:T(8,128)S(1)}, u32[]{:S(2)}, u32[]{:S(2)}) collective-permute-start(f32[256,128]{1,0:T(8,128)S(1)} %get-tuple-element.25), channel_id=1, source_target_pairs={{0,384},{128,256},{256,128},{384,0},{1,385},{129,257},{257,129},{3... | collective-permute-start | bytes 393224 | tf_op jit(solution)/shard_map/ppermute | solution.py:35
  86.9 5.9 %collective-permute-done.8.refs_3_ = f32[512,128]{1,0:T(8,128)S(1)} collective-permute-done((f32[512,128]{1,0:T(8,128)S(1)}, f32[512,128]{1,0:T(8,128)S(1)}, u32[]{:S(2)}, u32[]{:S(2)}) %collective-permute-start.8) | collective-permute-done | bytes 262176 | tf_op jit(solution)/shard_map/ppermute | solution.py:35
  93.2 2.4 %collective-permute-done.5.refs_3_ = f32[256,128]{1,0:T(8,128)S(1)} collective-permute-done((f32[256,128]{1,0:T(8,128)S(1)}, f32[256,128]{1,0:T(8,128)S(1)}, u32[]{:S(2)}, u32[]{:S(2)}) %collective-permute-start.5) | collective-permute-done | bytes 131104 | tf_op jit(solution)/shard_map/ppermute | solution.py:35
  95.6 2.7 %weight_sums.1 = f32[9,64,128]{2,1,0:T(8,128)} custom-call(s32[1]{0:T(128)} %bitcast.slab, f32[256,128]{1,0:T(8,128)S(1)} %get-tuple-element.22.refs_0_, f32[256,128]{1,0:T(8,128)S(1)} %collective-permute-done.3.refs_1_, f32[256,128]{1,0:T(8,128)S(1)} %collective-permute-done.4.refs_2_, f32[256,128]{1,0:T(8,128)S(1)} %collective-permute-done.5.refs_3_, ...), custom_call_target="tpu_custom_call" | custom-call | tf_op jit(solution)/shard_map/weight_sums/pallas_call | solution.py:318
  98.3 0.6 reduce_sum.9
  (15 shorter events, 1.5 us)
Async XLA Ops:
  1.5 6.8 %collective-permute-start = (f32[2,64,128]{2,1,0:T(8,128)S(1)}, f32[2,64,128]{2,1,0:T(8,128)S(1)}, u32[]{:S(2)}, u32[]{:S(2)}) collective-permute-start(f32[2,64,128]{2,1,0:T(8,128)S(1)} %get-tuple-element.27), channel_id=1, source_target_pairs={{0,128},{128,256},{256,384},{1,129},{129,257},{257,385},{2,130},{1... | collective-permute-start | bytes 196616 | tf_op jit(solution)/shard_map/ppermute | solution.py:30
  5.5 5.0 %collective-permute-start.1 = (f32[2,64,128]{2,1,0:T(8,128)S(1)}, f32[2,64,128]{2,1,0:T(8,128)S(1)}, u32[]{:S(2)}, u32[]{:S(2)}) collective-permute-start(f32[2,64,128]{2,1,0:T(8,128)S(1)} %get-tuple-element.26), channel_id=1, source_target_pairs={{128,0},{256,128},{384,256},{129,1},{257,129},{385,257},{130,2},{2... | collective-permute-start | bytes 196616 | tf_op jit(solution)/shard_map/ppermute | solution.py:30
  11.5 8.5 %collective-permute-start.2 = (f32[320,256]{1,0:T(8,128)S(1)}, f32[320,256]{1,0:T(8,128)S(1)}, u32[]{:S(2)}, u32[]{:S(2)}) collective-permute-start(f32[320,256]{1,0:T(8,128)S(1)} %get-tuple-element.20), channel_id=1, source_target_pairs={{0,1},{1,0},{2,3},{3,2},{4,5},{5,4},{6,7},{7,6},{8,9},{9,8},{10,11... | collective-permute-start | bytes 983048 | tf_op jit(solution)/shard_map/ppermute | solution.py:274
  19.7 7.9 %copy-start = (f32[3,3,256,128]{3,2,1,0:T(8,128)S(1)}, f32[3,3,256,128]{3,2,1,0:T(8,128)}, u32[]{:S(2)}) copy-start(f32[3,3,256,128]{3,2,1,0:T(8,128)} %param.6) | copy-start | bytes 3538948
  20.8 20.4 %all-to-all-start = ((f32[8,40,256]{2,1,0:T(8,128)}), f32[8,40,256]{2,1,0:T(8,128)S(1)}, u32[]{:S(2)}, u32[]{:S(2)}) async-start(f32[8,40,256]{2,1,0:T(8,128)} %bitcast.6), calls=%async_computation | async-start | bytes 655360 | tf_op jit(solution)/shard_map/all_to_all | solution.py:275
  58.7 9.0 %copy-start.1 = (f32[8,64,128]{2,1,0:T(8,128)S(1)}, f32[8,64,128]{2,1,0:T(8,128)}, u32[]{:S(2)}) copy-start(f32[8,64,128]{2,1,0:T(8,128)} %param.7) | copy-start | bytes 786436
  60.8 37.5 %all-to-all-start.1 = ((f32[8,8,8,128]{3,2,1,0:T(8,128)}), f32[8,8,8,128]{3,2,1,0:T(8,128)S(1)}, u32[]{:S(2)}, u32[]{:S(2)}) async-start(f32[8,8,8,128]{3,2,1,0:T(8,128)} %get-tuple-element.21), calls=%async_computation.1 | async-start | bytes 524288 | tf_op jit(solution)/shard_map/all_to_all | solution.py:308
  67.7 15.9 %collective-permute-start.6 = (f32[512,128]{1,0:T(8,128)S(1)}, f32[512,128]{1,0:T(8,128)S(1)}, u32[]{:S(2)}, u32[]{:S(2)}) collective-permute-start(f32[512,128]{1,0:T(8,128)S(1)} %bitcast.13), channel_id=1, source_target_pairs={{0,128},{128,0},{256,384},{384,256},{1,129},{129,1},{257,385},{385... | collective-permute-start | bytes 786440 | tf_op jit(solution)/shard_map/ppermute | solution.py:35
  70.8 16.1 %collective-permute-start.7 = (f32[512,128]{1,0:T(8,128)S(1)}, f32[512,128]{1,0:T(8,128)S(1)}, u32[]{:S(2)}, u32[]{:S(2)}) collective-permute-start(f32[512,128]{1,0:T(8,128)S(1)} %bitcast.14), channel_id=1, source_target_pairs={{0,256},{128,384},{256,0},{384,128},{1,257},{129,385},{257,1},{385... | collective-permute-start | bytes 786440 | tf_op jit(solution)/shard_map/ppermute | solution.py:35
  74.0 18.9 %collective-permute-start.8 = (f32[512,128]{1,0:T(8,128)S(1)}, f32[512,128]{1,0:T(8,128)S(1)}, u32[]{:S(2)}, u32[]{:S(2)}) collective-permute-start(f32[512,128]{1,0:T(8,128)S(1)} %bitcast.15), channel_id=1, source_target_pairs={{0,384},{128,256},{256,128},{384,0},{1,385},{129,257},{257,129},{3... | collective-permute-start | bytes 786440 | tf_op jit(solution)/shard_map/ppermute | solution.py:35
  77.3 15.9 %collective-permute-start.3 = (f32[256,128]{1,0:T(8,128)S(1)}, f32[256,128]{1,0:T(8,128)S(1)}, u32[]{:S(2)}, u32[]{:S(2)}) collective-permute-start(f32[256,128]{1,0:T(8,128)S(1)} %get-tuple-element.23), channel_id=1, source_target_pairs={{0,128},{128,0},{256,384},{384,256},{1,129},{129,1},{257,385},{385... | collective-permute-start | bytes 393224 | tf_op jit(solution)/shard_map/ppermute | solution.py:35
  79.2 14.0 %collective-permute-start.4 = (f32[256,128]{1,0:T(8,128)S(1)}, f32[256,128]{1,0:T(8,128)S(1)}, u32[]{:S(2)}, u32[]{:S(2)}) collective-permute-start(f32[256,128]{1,0:T(8,128)S(1)} %get-tuple-element.24), channel_id=1, source_target_pairs={{0,256},{128,384},{256,0},{384,128},{1,257},{129,385},{257,1},{385... | collective-permute-start | bytes 393224 | tf_op jit(solution)/shard_map/ppermute | solution.py:35
  83.6 12.1 %collective-permute-start.5 = (f32[256,128]{1,0:T(8,128)S(1)}, f32[256,128]{1,0:T(8,128)S(1)}, u32[]{:S(2)}, u32[]{:S(2)}) collective-permute-start(f32[256,128]{1,0:T(8,128)S(1)} %get-tuple-element.25), channel_id=1, source_target_pairs={{0,384},{128,256},{256,128},{384,0},{1,385},{129,257},{257,129},{3... | collective-permute-start | bytes 393224 | tf_op jit(solution)/shard_map/ppermute | solution.py:35

commit v5 on v4

--- a/solution.py
+++ b/solution.py
@@ -13,6 +13,7 @@
 HBM = pl.BlockSpec(memory_space=pltpu.HBM)
 SMEM = pl.BlockSpec(memory_space=pltpu.SMEM)
 CORES = 2
+STEPS = (0, 2, 1, 3)
 LIMIT = pltpu.CompilerParams(vmem_limit_bytes=24 * 2**20)
 
 
@@ -109,15 +110,6 @@
         top, rest = split(weight[tap])
         w_pair[tap // 3, (tap % 3) * depth : (tap % 3 + 1) * depth, :wide] = top
         w_pair[tap // 3, (tap % 3) * depth : (tap % 3 + 1) * depth, wide:] = rest
-
-
-def turn_grads(slab, *refs):
-    *grads, grad_t = refs
-    wide = grads[0].shape[1]
-    for step, grad in enumerate(grads):
-        top, rest = split(grad[...].T)
-        grad_t[slab[0] ^ step, :wide, :] = top
-        grad_t[slab[0] ^ step, wide:, :] = rest
 
 
 def activate(ends, pieces, own):
@@ -157,7 +149,7 @@
         else:
             second = swap_lanes(second)
         packed[quarter] = jnp.where(lower_lanes(first.shape), first, second)
-    for step, out in enumerate(local):
+    for step, out in zip(STEPS, local, strict=True):
         out[...] = packed[slab[0] ^ step]
     for row in range(rows + 2):
         store_taps(ordered[row * cols : (row + 1) * cols, :], high, low, row * cols)
@@ -177,42 +169,68 @@
             conv[block, row] = total[start : start + width, :]
 
 
-def weight_sums(cols, slab, *refs):
-    *local, grad_t, out, high, low = refs
-    slabs = len(local)
-    count, lanes = local[0].shape
-    part = lanes // 2
-    wide = out.shape[2]
-    blank = jnp.zeros((cols, 2 * lanes), BF16)
-    end = high.shape[0] - cols
-    for ref in (high, low):
-        ref[0:cols, :] = blank
-        ref[end : end + cols, :] = blank
+def pixel_sums(cols, source, grad_t, high, low):
+    count, lanes = source.shape
+    wide = grad_t.shape[1] // 2
+    for row in range(count // cols):
+        left, here, right = taps_of_row(source[row * cols : (row + 1) * cols, :])
+        lower = lower_lanes(here.shape)
+        pairs = (
+            (jnp.where(lower, left, swap_lanes(here)), right),
+            (jnp.where(lower, swap_lanes(left), here), swap_lanes(right)),
+        )
+        for half, pair in enumerate(pairs):
+            at = slice(half * count + row * cols, half * count + (row + 1) * cols)
+            for k, value in enumerate(pair):
+                top, rest = split(value)
+                high[at, k * lanes : (k + 1) * lanes] = top
+                low[at, k * lanes : (k + 1) * lanes] = rest
+    sums = []
+    for a in range(3):
+        both = dot(grad_t[a], high[...])
+        sums.append(both[:wide] + both[wide:] + dot(grad_t[a, :wide, :], low[...]))
+    return sums
+
+
+def early_sums(cols, slab, *refs):
+    *refs, out, grad_last, high, low, grad_t, whole, sems = refs
+    slabs = sems.shape[0]
+    grads, local = refs[:slabs], refs[slabs:]
+    pixels, wide = grads[0].shape
+    early = len(local)
+    copies = []
+    for step, grad in enumerate(grads):
+        start = pl.multiple_of(cols + (slab[0] ^ STEPS[step]) * pixels, cols)
+        copies.append(
+            pltpu.make_async_copy(grad, whole.at[pl.ds(start, pixels), :], sems.at[step])
+        )
+        copies[step].start()
+    blank = jnp.zeros((cols, wide), F32)
+    end = whole.shape[0] - cols
+    whole[0:cols, :] = blank
+    whole[end : end + cols, :] = blank
+    for copy in copies:
+        copy.wait()
+    for step in range(slabs):
+        into = grad_t.at[step] if step < early else grad_last.at[step - early]
+        for a in range(3):
+            start = pl.multiple_of((2 - a) * cols + (slab[0] ^ STEPS[step]) * pixels, cols)
+            top, rest = split(whole[pl.ds(start, pixels), :].T)
+            into[a, :wide, :] = top
+            into[a, wide:, :] = rest
     for step, source in enumerate(local):
-        base = cols + (slab[0] ^ step) * 2 * count
-        for row in range(count // cols):
-            left, here, right = taps_of_row(source[row * cols : (row + 1) * cols, :])
-            lower = lower_lanes(here.shape)
-            pairs = (
-                (jnp.where(lower, left, swap_lanes(here)), right),
-                (jnp.where(lower, swap_lanes(left), here), swap_lanes(right)),
-            )
-            for half, pair in enumerate(pairs):
-                start = pl.multiple_of(base + half * count + row * cols, cols)
-                for k, value in enumerate(pair):
-                    top, rest = split(value)
-                    high[pl.ds(start, cols), k * lanes : (k + 1) * lanes] = top
-                    low[pl.ds(start, cols), k * lanes : (k + 1) * lanes] = rest
+        for a, value in enumerate(pixel_sums(cols, source, grad_t.at[step], high, low)):
+            out[a] = value if step == 0 else out[a] + value
+
+
+def last_sums(cols, *refs):
+    *local, grad_t, sums, after, out, high, low = refs
+    part = out.shape[1]
+    terms = [
+        pixel_sums(cols, source, grad_t.at[step], high, low) for step, source in enumerate(local)
+    ]
     for a in range(3):
-        main = None
-        other = None
-        for j in range(slabs):
-            window = slice(a * cols + j * 2 * count, a * cols + (j + 1) * 2 * count)
-            one = dot(grad_t[j], high[window, :])
-            two = dot(grad_t[j, :wide, :], low[window, :])
-            main = one if main is None else main + one
-            other = two if other is None else other + two
-        turned = (main[:wide] + main[wide:] + other).T
+        turned = sum((term[a] for term in terms), sums[a]).T
         for b in range(3):
             out[a * 3 + b] = turned[b * part : (b + 1) * part, :]
 
@@ -274,7 +292,7 @@
     held = held + lax.ppermute(given, "core", [(0, 1), (1, 0)])
     pieces = lax.all_to_all(held.reshape(chips, chunk, mid), "chip", 0, 0, tiled=True)
     grads = [out_grad.reshape(rows * cols, wide)]
-    grads += [trade(grads[0], "slab", step) for step in range(1, slabs)]
+    grads += [trade(grads[0], "slab", step) for step in STEPS[1:]]
     low_end = jnp.where(slab == 0, cols, 0)
     high_end = jnp.where(slab == slabs - 1, ext - cols, ext)
     own = pl.pallas_call(
@@ -306,29 +324,38 @@
     )(slab[None], near(hidden), near(w_pair))
 
     gathered = lax.all_to_all(conv, "cout", 0, 0, tiled=True)
-    local[1:] = [trade(local[step], "slab", step) for step in range(1, slabs)]
-    grad_t = pl.pallas_call(
-        turn_grads,
-        out_shape=pltpu.VMEM((slabs, 2 * wide, rows * cols), BF16),
-        in_specs=[SMEM] + [VMEM] * slabs,
+    local[1:] = [trade(local[k], "slab", STEPS[k]) for k in range(1, slabs)]
+    output = jnp.sum(gathered, axis=0)
+    pixels = rows * cols
+    early = slabs // 2
+    tap_pair = [pltpu.VMEM((pixels, 2 * lanes), BF16)] * 2
+    sums, grad_last = pl.pallas_call(
+        functools.partial(early_sums, cols),
+        out_shape=[
+            pltpu.VMEM((3, wide, 2 * lanes), F32),
+            pltpu.VMEM((slabs - early, 3, 2 * wide, pixels), BF16),
+        ],
+        in_specs=[SMEM] + [HBM] * slabs + [VMEM] * early,
+        out_specs=[VMEM] * 2,
+        scratch_shapes=tap_pair
+        + [
+            pltpu.VMEM((early, 3, 2 * wide, pixels), BF16),
+            pltpu.VMEM((slabs * pixels + 2 * cols, wide), F32),
+            pltpu.SemaphoreType.DMA((slabs,)),
+        ],
+        name="early_sums",
+        compiler_params=LIMIT,
+    )(slab[None], *map(far, grads), *map(near, local[:early]))
+    weight_grad = pl.pallas_call(
+        functools.partial(last_sums, cols),
+        out_shape=jax.ShapeDtypeStruct((9, mid // slabs, wide), F32),
+        in_specs=[VMEM] * (slabs - early + 2) + [HBM],
         out_specs=VMEM,
-        name="turn_grads",
-        compiler_params=LIMIT,
-    )(slab[None], *map(near, grads))
-    weight_grad = pl.pallas_call(
-        functools.partial(weight_sums, cols),
-        out_shape=jax.ShapeDtypeStruct((9, mid // slabs, wide), F32),
-        in_specs=[SMEM] + [VMEM] * (slabs + 1),
-        out_specs=VMEM,
-        scratch_shapes=[
-            pltpu.VMEM(((slabs * rows + 2) * cols, 2 * lanes), BF16),
-            pltpu.VMEM(((slabs * rows + 2) * cols, 2 * lanes), BF16),
-        ],
-        name="weight_sums",
-        compiler_params=LIMIT,
-    )(slab[None], *map(near, local), near(grad_t))
+        scratch_shapes=tap_pair,
+        name="last_sums",
+        compiler_params=LIMIT,
+    )(*map(near, (*local[early:], grad_last, sums)), far(output))
     weight_grad = weight_grad.reshape(3, 3, mid // slabs, wide)
-    output = jnp.sum(gathered, axis=0)
     return (output, weight_grad)
 
 

time: 99.6 us -> 93.9 us (0.943)
  the two profiles are of different devices: /device:TPU:1 before, /device:TPU:8 now
where the time goes in v5:
time: 93.9 us; the launch traced here: 93.3 us
  starting transfers between devices  44.2 us (47%)
  waiting for transfers between devices  18.8 us (20%)
  blocking collectives  16.5 us (18%)
  Pallas kernels  10.6 us (11%)
  other arithmetic  1.48 us (2%)
    ppermute x6, starting transfers between devices, trade(): return lax.ppermute(value, axis, [(i, i ^ step) for i in range(count)])  19.7 us
    all_gather x1, blocking collectives, block(): hidden = lax.all_gather(own, ('chip', 'core'), axis=0, tiled=False)  16.5 us
    all_to_all x1, waiting for transfers between devices, block(): lax.all_to_all(held.reshape(chips, chunk, mid), 'chip', 0, 0, tiled=True)  13.3 us
    all_to_all x1, starting transfers between devices, block(): lax.all_to_all(held.reshape(chips, chunk, mid), 'chip', 0, 0, tiled=True)  10.3 us
    all_to_all x1, starting transfers between devices, block(): gathered = lax.all_to_all(conv, 'cout', 0, 0, tiled=True)  7.55 us
    ppermute x2, starting transfers between devices, shift(): return lax.ppermute(value, axis, pairs)  4.69 us
    ppermute x2, waiting for transfers between devices, shift(): return lax.ppermute(value, axis, pairs)  3.32 us
    pallas_call x1, Pallas kernels, block(): pl.pallas_call(functools.partial(early_sums, cols), out_shape=[pltpu.VMEM...  2.45 us
  transfers between devices with their start and end apart: 11, of which 6 were waited for; matrix products, arithmetic and copies ran while one was open for 1% of the time, Pallas kernels for 5%

profile of v5, /device:TPU:8, one launch (start us, length us, event | category | flops | bytes accessed | tf_op | source)
XLA Modules:
  0.0 93.3 jit_solution(7637831330673132564)
XLA Ops:
  0.6 0.9 fusion
  1.5 3.4 %collective-permute-start = (f32[2,64,128]{2,1,0:T(8,128)S(1)}, f32[2,64,128]{2,1,0:T(8,128)S(1)}, u32[]{:S(2)}, u32[]{:S(2)}) collective-permute-start(f32[2,64,128]{2,1,0:T(8,128)S(1)} %get-tuple-element.31), channel_id=1, source_target_pairs={{0,128},{128,256},{256,384},{1,129},{129,257},{257,385},{2,130},{1... | collective-permute-start | bytes 196616 | tf_op jit(solution)/shard_map/ppermute | solution.py:31
  4.9 1.3 %collective-permute-start.1 = (f32[2,64,128]{2,1,0:T(8,128)S(1)}, f32[2,64,128]{2,1,0:T(8,128)S(1)}, u32[]{:S(2)}, u32[]{:S(2)}) collective-permute-start(f32[2,64,128]{2,1,0:T(8,128)S(1)} %get-tuple-element.30), channel_id=1, source_target_pairs={{128,0},{256,128},{384,256},{129,1},{257,129},{385,257},{130,2},{2... | collective-permute-start | bytes 196616 | tf_op jit(solution)/shard_map/ppermute | solution.py:31
  6.2 1.5 %first_prepare.1 = (bf16[512,384]{1,0:T(8,128)(2,1)S(1)}, bf16[512,384]{1,0:T(8,128)(2,1)S(1)}, bf16[3,384,256]{2,1,0:T(8,128)(2,1)S(1)}, bf16[3,384,256]{2,1,0:T(8,128)(2,1)S(1)}) custom-call(f32[8,64,128]{2,1,0:T(8,128)} %image.1, f32[9,128,256]{2,1,0:T(8,128)} %bitcast.13), custom_call_target="tpu_custom_call" | custom-call | tf_op jit(solution)/shard_map/first_prepare/pallas_call | solution.py:253
  7.8 3.3 %collective-permute-done.1.below = f32[2,64,128]{2,1,0:T(8,128)S(1)} collective-permute-done((f32[2,64,128]{2,1,0:T(8,128)S(1)}, f32[2,64,128]{2,1,0:T(8,128)S(1)}, u32[]{:S(2)}, u32[]{:S(2)}) %collective-permute-start.1) | collective-permute-done | bytes 65568 | tf_op jit(solution)/shard_map/ppermute | solution.py:31
  11.1 1.0 %first_given.1 = (f32[320,256]{1,0:T(8,128)S(1)}, bf16[768,384]{1,0:T(8,128)(2,1)S(1)}, bf16[768,384]{1,0:T(8,128)(2,1)S(1)}) custom-call(s32[1]{0:T(128)} %bitcast.4.core, f32[2,64,128]{2,1,0:T(8,128)S(1)} %collective-permute-done.above, f32[2,64,128]{2,1,0:T(8,128)S(1)} %collective-permute-done.1.below, bf16[512,384]{1,0:T(8,128)(2,1)S(1)} %get-tuple-element.16.high_in, ...), custom_call_target="tpu_custom_call" | custom-call | tf_op jit(solution)/shard_map/first_given/pallas_call | solution.py:266
  12.1 1.9 %collective-permute-start.2 = (f32[320,256]{1,0:T(8,128)S(1)}, f32[320,256]{1,0:T(8,128)S(1)}, u32[]{:S(2)}, u32[]{:S(2)}) collective-permute-start(f32[320,256]{1,0:T(8,128)S(1)} %get-tuple-element.22), channel_id=1, source_target_pairs={{0,1},{1,0},{2,3},{3,2},{4,5},{5,4},{6,7},{7,6},{8,9},{9,8},{10,11... | collective-permute-start | bytes 983048 | tf_op jit(solution)/shard_map/ppermute | solution.py:292
  14.0 0.9 first_held.1
  15.0 0.7 collective-permute-done.2
  15.6 0.8 add.7
  16.4 10.3 %all-to-all-start = ((f32[8,40,256]{2,1,0:T(8,128)}), f32[8,40,256]{2,1,0:T(8,128)S(1)}, u32[]{:S(2)}, u32[]{:S(2)}) async-start(f32[8,40,256]{2,1,0:T(8,128)} %bitcast.6), calls=%async_computation | async-start | bytes 655360 | tf_op jit(solution)/shard_map/all_to_all | solution.py:293
  27.0 13.3 %all-to-all-done.pieces = f32[8,40,256]{2,1,0:T(8,128)S(1)} async-done(((f32[8,40,256]{2,1,0:T(8,128)}), f32[8,40,256]{2,1,0:T(8,128)S(1)}, u32[]{:S(2)}, u32[]{:S(2)}) %all-to-all-start) | async-done | bytes 327712 | tf_op jit(solution)/shard_map/all_to_all | solution.py:293
  40.9 16.5 %all-gather = f32[640,256]{1,0:T(8,128)S(1)} all-gather(f32[40,256]{1,0:T(8,128)S(1)} %activate.1), channel_id=2, replica_groups=mesh['slab'=4,'cout'=8,'chip'=8,'core'=2] {'chip','core'}, dimensions={0}, use_global_device_ids=true | all-gather | bytes 696320 | tf_op jit(solution)/shard_map/all_gather | solution.py:306
  57.4 2.1 %second_conv.1 = (f32[8,8,8,128]{3,2,1,0:T(8,128)}, f32[256,128]{1,0:T(8,128)S(1)}, f32[256,128]{1,0:T(8,128)S(1)}, f32[256,128]{1,0:T(8,128)S(1)}, f32[256,128]{1,0:T(8,128)S(1)}) custom-call(s32[1]{0:T(128)} %bitcast.slab, f32[16,40,256]{2,1,0:T(8,128)S(1)} %bitcast.11, bf16[3,768,256]{2,1,0:T(8,128)(2,1)S(1)} %prepare.1.w_pair), custom_call_target="tpu_custom_call" | custom-call | tf_op jit(solution)/shard_map/second_conv/pallas_call | solution.py:310
  59.5 7.5 %all-to-all-start.1 = ((f32[8,8,8,128]{3,2,1,0:T(8,128)}), f32[8,8,8,128]{3,2,1,0:T(8,128)S(1)}, u32[]{:S(2)}, u32[]{:S(2)}) async-start(f32[8,8,8,128]{3,2,1,0:T(8,128)} %get-tuple-element.23), calls=%async_computation.1 | async-start | bytes 524288 | tf_op jit(solution)/shard_map/all_to_all | solution.py:326
  67.1 4.6 %collective-permute-start.5 = (f32[512,128]{1,0:T(8,128)S(1)}, f32[512,128]{1,0:T(8,128)S(1)}, u32[]{:S(2)}, u32[]{:S(2)}) collective-permute-start(f32[512,128]{1,0:T(8,128)S(1)} %bitcast.16), channel_id=1, source_target_pairs={{0,256},{128,384},{256,0},{384,128},{1,257},{129,385},{257,1},{385... | collective-permute-start | bytes 786440 | tf_op jit(solution)/shard_map/ppermute | solution.py:36
  71.7 1.9 %collective-permute-start.6 = (f32[512,128]{1,0:T(8,128)S(1)}, f32[512,128]{1,0:T(8,128)S(1)}, u32[]{:S(2)}, u32[]{:S(2)}) collective-permute-start(f32[512,128]{1,0:T(8,128)S(1)} %bitcast.17), channel_id=1, source_target_pairs={{0,128},{128,0},{256,384},{384,256},{1,129},{129,1},{257,385},{385... | collective-permute-start | bytes 786440 | tf_op jit(solution)/shard_map/ppermute | solution.py:36
  73.6 3.3 %collective-permute-start.7 = (f32[512,128]{1,0:T(8,128)S(1)}, f32[512,128]{1,0:T(8,128)S(1)}, u32[]{:S(2)}, u32[]{:S(2)}) collective-permute-start(f32[512,128]{1,0:T(8,128)S(1)} %bitcast.18), channel_id=1, source_target_pairs={{0,384},{128,256},{256,128},{384,0},{1,385},{129,257},{257,129},{3... | collective-permute-start | bytes 786440 | tf_op jit(solution)/shard_map/ppermute | solution.py:36
  77.0 4.6 %collective-permute-start.8 = (f32[256,128]{1,0:T(8,128)S(1)}, f32[256,128]{1,0:T(8,128)S(1)}, u32[]{:S(2)}, u32[]{:S(2)}) collective-permute-start(f32[256,128]{1,0:T(8,128)S(1)} %get-tuple-element.27), channel_id=1, source_target_pairs={{0,256},{128,384},{256,0},{384,128},{1,257},{129,385},{257,1},{385... | collective-permute-start | bytes 393224 | tf_op jit(solution)/shard_map/ppermute | solution.py:36
  81.6 1.9 %collective-permute-start.3 = (f32[256,128]{1,0:T(8,128)S(1)}, f32[256,128]{1,0:T(8,128)S(1)}, u32[]{:S(2)}, u32[]{:S(2)}) collective-permute-start(f32[256,128]{1,0:T(8,128)S(1)} %get-tuple-element.24), channel_id=1, source_target_pairs={{0,128},{128,0},{256,384},{384,256},{1,129},{129,1},{257,385},{385... | collective-permute-start | bytes 393224 | tf_op jit(solution)/shard_map/ppermute | solution.py:36
  83.5 3.3 %collective-permute-start.4 = (f32[256,128]{1,0:T(8,128)S(1)}, f32[256,128]{1,0:T(8,128)S(1)}, u32[]{:S(2)}, u32[]{:S(2)}) collective-permute-start(f32[256,128]{1,0:T(8,128)S(1)} %get-tuple-element.25), channel_id=1, source_target_pairs={{0,384},{128,256},{256,128},{384,0},{1,385},{129,257},{257,129},{3... | collective-permute-start | bytes 393224 | tf_op jit(solution)/shard_map/ppermute | solution.py:36
  87.3 0.8 collective-permute-done.8.refs_5_
  88.1 2.5 %early_sums.1 = (f32[3,128,256]{2,1,0:T(8,128)S(1)}, bf16[2,3,256,512]{3,2,1,0:T(8,128)(2,1)S(1)}) custom-call(s32[1]{0:T(128)} %bitcast.slab, f32[512,128]{1,0:T(8,128)} %bitcast.15, f32[512,128]{1,0:T(8,128)} %copy-done.2, f32[512,128]{1,0:T(8,128)} %copy-done.3, f32[512,128]{1,0:T(8,128)} %copy-done.4, f32[256,128]{1,0:T(8,128)S(1)} %get-tuple-element.26.refs_4_, ...), custom_call_target="tpu_custom_call" | custom-call | tf_op jit(solution)/shard_map/early_sums/pallas_call | solution.py:332
  91.6 1.7 %last_sums.1 = f32[9,64,128]{2,1,0:T(8,128)} custom-call(f32[256,128]{1,0:T(8,128)S(1)} %collective-permute-done.3.refs_0_, f32[256,128]{1,0:T(8,128)S(1)} %collective-permute-done.4.refs_1_, bf16[2,3,256,512]{3,2,1,0:T(8,128)(2,1)S(1)} %get-tuple-element.28.refs_2_, f32[3,128,256]{2,1,0:T(8,128)S(1)} %get-tuple-element.29.refs_3_, ...), custom_call_target="tpu_custom_call" | custom-call | tf_op jit(solution)/shard_map/last_sums/pallas_call | solution.py:349
  (21 shorter events, 2.3 us)
Async XLA Ops:
  1.5 6.2 %collective-permute-start = (f32[2,64,128]{2,1,0:T(8,128)S(1)}, f32[2,64,128]{2,1,0:T(8,128)S(1)}, u32[]{:S(2)}, u32[]{:S(2)}) collective-permute-start(f32[2,64,128]{2,1,0:T(8,128)S(1)} %get-tuple-element.31), channel_id=1, source_target_pairs={{0,128},{128,256},{256,384},{1,129},{129,257},{257,385},{2,130},{1... | collective-permute-start | bytes 196616 | tf_op jit(solution)/shard_map/ppermute | solution.py:31
  4.9 6.2 %collective-permute-start.1 = (f32[2,64,128]{2,1,0:T(8,128)S(1)}, f32[2,64,128]{2,1,0:T(8,128)S(1)}, u32[]{:S(2)}, u32[]{:S(2)}) collective-permute-start(f32[2,64,128]{2,1,0:T(8,128)S(1)} %get-tuple-element.30), channel_id=1, source_target_pairs={{128,0},{256,128},{384,256},{129,1},{257,129},{385,257},{130,2},{2... | collective-permute-start | bytes 196616 | tf_op jit(solution)/shard_map/ppermute | solution.py:31
  12.1 3.5 %collective-permute-start.2 = (f32[320,256]{1,0:T(8,128)S(1)}, f32[320,256]{1,0:T(8,128)S(1)}, u32[]{:S(2)}, u32[]{:S(2)}) collective-permute-start(f32[320,256]{1,0:T(8,128)S(1)} %get-tuple-element.22), channel_id=1, source_target_pairs={{0,1},{1,0},{2,3},{3,2},{4,5},{5,4},{6,7},{7,6},{8,9},{9,8},{10,11... | collective-permute-start | bytes 983048 | tf_op jit(solution)/shard_map/ppermute | solution.py:292
  15.0 11.8 %copy-start = (f32[3,3,256,128]{3,2,1,0:T(8,128)S(1)}, f32[3,3,256,128]{3,2,1,0:T(8,128)}, u32[]{:S(2)}) copy-start(f32[3,3,256,128]{3,2,1,0:T(8,128)} %param.6) | copy-start | bytes 3538948
  16.4 23.9 %all-to-all-start = ((f32[8,40,256]{2,1,0:T(8,128)}), f32[8,40,256]{2,1,0:T(8,128)S(1)}, u32[]{:S(2)}, u32[]{:S(2)}) async-start(f32[8,40,256]{2,1,0:T(8,128)} %bitcast.6), calls=%async_computation | async-start | bytes 655360 | tf_op jit(solution)/shard_map/all_to_all | solution.py:293
  57.4 9.7 %copy-start.1 = (f32[8,64,128]{2,1,0:T(8,128)S(1)}, f32[8,64,128]{2,1,0:T(8,128)}, u32[]{:S(2)}) copy-start(f32[8,64,128]{2,1,0:T(8,128)} %param.7) | copy-start | bytes 786436
  59.5 31.0 %all-to-all-start.1 = ((f32[8,8,8,128]{3,2,1,0:T(8,128)}), f32[8,8,8,128]{3,2,1,0:T(8,128)S(1)}, u32[]{:S(2)}, u32[]{:S(2)}) async-start(f32[8,8,8,128]{3,2,1,0:T(8,128)} %get-tuple-element.23), calls=%async_computation.1 | async-start | bytes 524288 | tf_op jit(solution)/shard_map/all_to_all | solution.py:326
  67.1 16.4 %collective-permute-start.5 = (f32[512,128]{1,0:T(8,128)S(1)}, f32[512,128]{1,0:T(8,128)S(1)}, u32[]{:S(2)}, u32[]{:S(2)}) collective-permute-start(f32[512,128]{1,0:T(8,128)S(1)} %bitcast.16), channel_id=1, source_target_pairs={{0,256},{128,384},{256,0},{384,128},{1,257},{129,385},{257,1},{385... | collective-permute-start | bytes 786440 | tf_op jit(solution)/shard_map/ppermute | solution.py:36
  71.7 15.1 %collective-permute-start.6 = (f32[512,128]{1,0:T(8,128)S(1)}, f32[512,128]{1,0:T(8,128)S(1)}, u32[]{:S(2)}, u32[]{:S(2)}) collective-permute-start(f32[512,128]{1,0:T(8,128)S(1)} %bitcast.17), channel_id=1, source_target_pairs={{0,128},{128,0},{256,384},{384,256},{1,129},{129,1},{257,385},{385... | collective-permute-start | bytes 786440 | tf_op jit(solution)/shard_map/ppermute | solution.py:36
  73.6 13.6 %collective-permute-start.7 = (f32[512,128]{1,0:T(8,128)S(1)}, f32[512,128]{1,0:T(8,128)S(1)}, u32[]{:S(2)}, u32[]{:S(2)}) collective-permute-start(f32[512,128]{1,0:T(8,128)S(1)} %bitcast.18), channel_id=1, source_target_pairs={{0,384},{128,256},{256,128},{384,0},{1,385},{129,257},{257,129},{3... | collective-permute-start | bytes 786440 | tf_op jit(solution)/shard_map/ppermute | solution.py:36
  77.0 11.1 %collective-permute-start.8 = (f32[256,128]{1,0:T(8,128)S(1)}, f32[256,128]{1,0:T(8,128)S(1)}, u32[]{:S(2)}, u32[]{:S(2)}) collective-permute-start(f32[256,128]{1,0:T(8,128)S(1)} %get-tuple-element.27), channel_id=1, source_target_pairs={{0,256},{128,384},{256,0},{384,128},{1,257},{129,385},{257,1},{385... | collective-permute-start | bytes 393224 | tf_op jit(solution)/shard_map/ppermute | solution.py:36
  81.6 9.6 %collective-permute-start.3 = (f32[256,128]{1,0:T(8,128)S(1)}, f32[256,128]{1,0:T(8,128)S(1)}, u32[]{:S(2)}, u32[]{:S(2)}) collective-permute-start(f32[256,128]{1,0:T(8,128)S(1)} %get-tuple-element.24), channel_id=1, source_target_pairs={{0,128},{128,0},{256,384},{384,256},{1,129},{129,1},{257,385},{385... | collective-permute-start | bytes 393224 | tf_op jit(solution)/shard_map/ppermute | solution.py:36
  83.5 4.6 %copy-start.2 = (f32[512,128]{1,0:T(8,128)}, f32[512,128]{1,0:T(8,128)S(1)}, u32[]{:S(2)}) copy-start(f32[512,128]{1,0:T(8,128)S(1)} %collective-permute-done.5.refs_1_) | copy-start | bytes 786436
  83.5 8.1 %collective-permute-start.4 = (f32[256,128]{1,0:T(8,128)S(1)}, f32[256,128]{1,0:T(8,128)S(1)}, u32[]{:S(2)}, u32[]{:S(2)}) collective-permute-start(f32[256,128]{1,0:T(8,128)S(1)} %get-tuple-element.25), channel_id=1, source_target_pairs={{0,384},{128,256},{256,128},{384,0},{1,385},{129,257},{257,129},{3... | collective-permute-start | bytes 393224 | tf_op jit(solution)/shard_map/ppermute | solution.py:36
  86.9 1.2 %copy-start.3 = (f32[512,128]{1,0:T(8,128)}, f32[512,128]{1,0:T(8,128)S(1)}, u32[]{:S(2)}) copy-start(f32[512,128]{1,0:T(8,128)S(1)} %collective-permute-done.6.refs_2_) | copy-start | bytes 786436
  87.3 0.8 copy-start.4

commit v6 on v5

--- a/solution.py
+++ b/solution.py
@@ -169,9 +169,8 @@
             conv[block, row] = total[start : start + width, :]
 
 
-def pixel_sums(cols, source, grad_t, high, low):
+def pixel_taps(cols, source, high, low):
     count, lanes = source.shape
-    wide = grad_t.shape[1] // 2
     for row in range(count // cols):
         left, here, right = taps_of_row(source[row * cols : (row + 1) * cols, :])
         lower = lower_lanes(here.shape)
@@ -185,6 +184,10 @@
                 top, rest = split(value)
                 high[at, k * lanes : (k + 1) * lanes] = top
                 low[at, k * lanes : (k + 1) * lanes] = rest
+
+
+def pixel_sums(grad_t, high, low):
+    wide = grad_t.shape[1] // 2
     sums = []
     for a in range(3):
         both = dot(grad_t[a], high[...])
@@ -196,43 +199,48 @@
     *refs, out, grad_last, high, low, grad_t, whole, sems = refs
     slabs = sems.shape[0]
     grads, local = refs[:slabs], refs[slabs:]
-    pixels, wide = grads[0].shape
+    rows, _, wide = grads[0].shape
     early = len(local)
     copies = []
     for step, grad in enumerate(grads):
-        start = pl.multiple_of(cols + (slab[0] ^ STEPS[step]) * pixels, cols)
-        copies.append(
-            pltpu.make_async_copy(grad, whole.at[pl.ds(start, pixels), :], sems.at[step])
-        )
+        into = whole.at[pl.ds(1 + (slab[0] ^ STEPS[step]) * rows, rows)]
+        copies.append(pltpu.make_async_copy(grad, into, sems.at[step]))
         copies[step].start()
     blank = jnp.zeros((cols, wide), F32)
-    end = whole.shape[0] - cols
-    whole[0:cols, :] = blank
-    whole[end : end + cols, :] = blank
+    whole[0] = blank
+    whole[whole.shape[0] - 1] = blank
+    for step, source in enumerate(local):
+        pixel_taps(cols, source, high.at[step], low.at[step])
     for copy in copies:
         copy.wait()
     for step in range(slabs):
         into = grad_t.at[step] if step < early else grad_last.at[step - early]
         for a in range(3):
-            start = pl.multiple_of((2 - a) * cols + (slab[0] ^ STEPS[step]) * pixels, cols)
-            top, rest = split(whole[pl.ds(start, pixels), :].T)
+            window = whole[pl.ds((slab[0] ^ STEPS[step]) * rows + 2 - a, rows)]
+            top, rest = split(window.reshape(rows * cols, wide).T)
             into[a, :wide, :] = top
             into[a, wide:, :] = rest
+    for step in range(early):
+        sums = pixel_sums(grad_t.at[step], high.at[step], low.at[step])
+        for a, value in enumerate(sums):
+            out[a] = value if step == 0 else out[a] + value
+
+
+def last_sums(cols, *refs):
+    *local, grad_t, sums, gathered, out, output, high, low = refs
+    part = out.shape[1]
+    terms = []
     for step, source in enumerate(local):
-        for a, value in enumerate(pixel_sums(cols, source, grad_t.at[step], high, low)):
-            out[a] = value if step == 0 else out[a] + value
-
-
-def last_sums(cols, *refs):
-    *local, grad_t, sums, after, out, high, low = refs
-    part = out.shape[1]
-    terms = [
-        pixel_sums(cols, source, grad_t.at[step], high, low) for step, source in enumerate(local)
-    ]
+        pixel_taps(cols, source, high.at[step], low.at[step])
+        terms.append(pixel_sums(grad_t.at[step], high.at[step], low.at[step]))
     for a in range(3):
         turned = sum((term[a] for term in terms), sums[a]).T
         for b in range(3):
             out[a * 3 + b] = turned[b * part : (b + 1) * part, :]
+    total = gathered[0]
+    for piece in range(1, gathered.shape[0]):
+        total += gathered[piece]
+    output[...] = total
 
 
 def block(image_in, first_weight, second_weight, out_grad):
@@ -291,7 +299,7 @@
 
     held = held + lax.ppermute(given, "core", [(0, 1), (1, 0)])
     pieces = lax.all_to_all(held.reshape(chips, chunk, mid), "chip", 0, 0, tiled=True)
-    grads = [out_grad.reshape(rows * cols, wide)]
+    grads = [out_grad]
     grads += [trade(grads[0], "slab", step) for step in STEPS[1:]]
     low_end = jnp.where(slab == 0, cols, 0)
     high_end = jnp.where(slab == slabs - 1, ext - cols, ext)
@@ -325,10 +333,9 @@
 
     gathered = lax.all_to_all(conv, "cout", 0, 0, tiled=True)
     local[1:] = [trade(local[k], "slab", STEPS[k]) for k in range(1, slabs)]
-    output = jnp.sum(gathered, axis=0)
     pixels = rows * cols
     early = slabs // 2
-    tap_pair = [pltpu.VMEM((pixels, 2 * lanes), BF16)] * 2
+    tap_pair = [pltpu.VMEM((early, pixels, 2 * lanes), BF16)] * 2
     sums, grad_last = pl.pallas_call(
         functools.partial(early_sums, cols),
         out_shape=[
@@ -340,21 +347,24 @@
         scratch_shapes=tap_pair
         + [
             pltpu.VMEM((early, 3, 2 * wide, pixels), BF16),
-            pltpu.VMEM((slabs * pixels + 2 * cols, wide), F32),
+            pltpu.VMEM((slabs * rows + 2, cols, wide), F32),
             pltpu.SemaphoreType.DMA((slabs,)),
         ],
         name="early_sums",
         compiler_params=LIMIT,
     )(slab[None], *map(far, grads), *map(near, local[:early]))
-    weight_grad = pl.pallas_call(
+    weight_grad, output = pl.pallas_call(
         functools.partial(last_sums, cols),
-        out_shape=jax.ShapeDtypeStruct((9, mid // slabs, wide), F32),
-        in_specs=[VMEM] * (slabs - early + 2) + [HBM],
-        out_specs=VMEM,
+        out_shape=[
+            jax.ShapeDtypeStruct((9, mid // slabs, wide), F32),
+            jax.ShapeDtypeStruct((rows, cols // n_out, wide), F32),
+        ],
+        in_specs=[VMEM] * (slabs - early + 3),
+        out_specs=[VMEM] * 2,
         scratch_shapes=tap_pair,
         name="last_sums",
         compiler_params=LIMIT,
-    )(*map(near, (*local[early:], grad_last, sums)), far(output))
+    )(*map(near, (*local[early:], grad_last, sums, gathered)))
     weight_grad = weight_grad.reshape(3, 3, mid // slabs, wide)
     return (output, weight_grad)
 

time: 93.9 us -> 93.9 us (level)
  transfers between devices with their start and end apart: 11 -> 11, of which waited for: 6 -> 6; matrix products, arithmetic and copies ran while one was open for 1% -> 0% of each run, Pallas kernels for 5% -> 5%
where the time goes in v6:
time: 93.9 us; the launch traced here: 93.3 us
  starting transfers between devices  44.2 us (47%)
  waiting for transfers between devices  19.6 us (21%)
  blocking collectives  16.5 us (18%)
  Pallas kernels  10.5 us (11%)
    ppermute x6, starting transfers between devices, trade(): return lax.ppermute(value, axis, [(i, i ^ step) for i in range(count)])  19.7 us
    all_gather x1, blocking collectives, block(): hidden = lax.all_gather(own, ('chip', 'core'), axis=0, tiled=False)  16.5 us
    all_to_all x1, waiting for transfers between devices, block(): lax.all_to_all(held.reshape(chips, chunk, mid), 'chip', 0, 0, tiled=True)  13.3 us
    all_to_all x1, starting transfers between devices, block(): lax.all_to_all(held.reshape(chips, chunk, mid), 'chip', 0, 0, tiled=True)  10.3 us
    all_to_all x1, starting transfers between devices, block(): gathered = lax.all_to_all(conv, 'cout', 0, 0, tiled=True)  7.55 us
    ppermute x2, starting transfers between devices, shift(): return lax.ppermute(value, axis, pairs)  4.69 us
    ppermute x2, waiting for transfers between devices, shift(): return lax.ppermute(value, axis, pairs)  3.32 us
    pallas_call x1, Pallas kernels, block(): pl.pallas_call(functools.partial(early_sums, cols), out_shape=[pltpu.VMEM...  2.36 us
  transfers between devices with their start and end apart: 11, of which 6 were waited for; matrix products, arithmetic and copies ran while one was open for 0% of the time, Pallas kernels for 5%

profile of v6, /device:TPU:8, one launch (start us, length us, event | category | flops | bytes accessed | tf_op | source)
XLA Modules:
  0.0 93.3 jit_solution(960497928981464167)
XLA Ops:
  0.6 0.9 fusion
  1.5 3.4 %collective-permute-start = (f32[2,64,128]{2,1,0:T(8,128)S(1)}, f32[2,64,128]{2,1,0:T(8,128)S(1)}, u32[]{:S(2)}, u32[]{:S(2)}) collective-permute-start(f32[2,64,128]{2,1,0:T(8,128)S(1)} %get-tuple-element.35), channel_id=1, source_target_pairs={{0,128},{128,256},{256,384},{1,129},{129,257},{257,385},{2,130},{1... | collective-permute-start | bytes 196616 | tf_op jit(solution)/shard_map/ppermute | solution.py:31
  4.9 1.3 %collective-permute-start.1 = (f32[2,64,128]{2,1,0:T(8,128)S(1)}, f32[2,64,128]{2,1,0:T(8,128)S(1)}, u32[]{:S(2)}, u32[]{:S(2)}) collective-permute-start(f32[2,64,128]{2,1,0:T(8,128)S(1)} %get-tuple-element.34), channel_id=1, source_target_pairs={{128,0},{256,128},{384,256},{129,1},{257,129},{385,257},{130,2},{2... | collective-permute-start | bytes 196616 | tf_op jit(solution)/shard_map/ppermute | solution.py:31
  6.2 1.5 %first_prepare.1 = (bf16[512,384]{1,0:T(8,128)(2,1)S(1)}, bf16[512,384]{1,0:T(8,128)(2,1)S(1)}, bf16[3,384,256]{2,1,0:T(8,128)(2,1)S(1)}, bf16[3,384,256]{2,1,0:T(8,128)(2,1)S(1)}) custom-call(f32[8,64,128]{2,1,0:T(8,128)} %image.1, f32[9,128,256]{2,1,0:T(8,128)} %bitcast.12), custom_call_target="tpu_custom_call" | custom-call | tf_op jit(solution)/shard_map/first_prepare/pallas_call | solution.py:261
  7.8 3.3 %collective-permute-done.1.below = f32[2,64,128]{2,1,0:T(8,128)S(1)} collective-permute-done((f32[2,64,128]{2,1,0:T(8,128)S(1)}, f32[2,64,128]{2,1,0:T(8,128)S(1)}, u32[]{:S(2)}, u32[]{:S(2)}) %collective-permute-start.1) | collective-permute-done | bytes 65568 | tf_op jit(solution)/shard_map/ppermute | solution.py:31
  11.1 1.0 %first_given.1 = (f32[320,256]{1,0:T(8,128)S(1)}, bf16[768,384]{1,0:T(8,128)(2,1)S(1)}, bf16[768,384]{1,0:T(8,128)(2,1)S(1)}) custom-call(s32[1]{0:T(128)} %bitcast.4.core, f32[2,64,128]{2,1,0:T(8,128)S(1)} %collective-permute-done.above, f32[2,64,128]{2,1,0:T(8,128)S(1)} %collective-permute-done.1.below, bf16[512,384]{1,0:T(8,128)(2,1)S(1)} %get-tuple-element.18.high_in, ...), custom_call_target="tpu_custom_call" | custom-call | tf_op jit(solution)/shard_map/first_given/pallas_call | solution.py:274
  12.1 1.9 %collective-permute-start.2 = (f32[320,256]{1,0:T(8,128)S(1)}, f32[320,256]{1,0:T(8,128)S(1)}, u32[]{:S(2)}, u32[]{:S(2)}) collective-permute-start(f32[320,256]{1,0:T(8,128)S(1)} %get-tuple-element.24), channel_id=1, source_target_pairs={{0,1},{1,0},{2,3},{3,2},{4,5},{5,4},{6,7},{7,6},{8,9},{9,8},{10,11... | collective-permute-start | bytes 983048 | tf_op jit(solution)/shard_map/ppermute | solution.py:300
  14.0 0.9 first_held.1
  15.6 0.8 add.7
  16.4 10.3 %all-to-all-start = ((f32[8,40,256]{2,1,0:T(8,128)}), f32[8,40,256]{2,1,0:T(8,128)S(1)}, u32[]{:S(2)}, u32[]{:S(2)}) async-start(f32[8,40,256]{2,1,0:T(8,128)} %bitcast.6), calls=%async_computation | async-start | bytes 655360 | tf_op jit(solution)/shard_map/all_to_all | solution.py:301
  27.0 13.3 %all-to-all-done.pieces = f32[8,40,256]{2,1,0:T(8,128)S(1)} async-done(((f32[8,40,256]{2,1,0:T(8,128)}), f32[8,40,256]{2,1,0:T(8,128)S(1)}, u32[]{:S(2)}, u32[]{:S(2)}) %all-to-all-start) | async-done | bytes 327712 | tf_op jit(solution)/shard_map/all_to_all | solution.py:301
  40.9 16.5 %all-gather = f32[640,256]{1,0:T(8,128)S(1)} all-gather(f32[40,256]{1,0:T(8,128)S(1)} %activate.1), channel_id=2, replica_groups=mesh['slab'=4,'cout'=8,'chip'=8,'core'=2] {'chip','core'}, dimensions={0}, use_global_device_ids=true | all-gather | bytes 696320 | tf_op jit(solution)/shard_map/all_gather | solution.py:314
  57.4 2.1 %second_conv.1 = (f32[8,8,8,128]{3,2,1,0:T(8,128)}, f32[256,128]{1,0:T(8,128)S(1)}, f32[256,128]{1,0:T(8,128)S(1)}, f32[256,128]{1,0:T(8,128)S(1)}, f32[256,128]{1,0:T(8,128)S(1)}) custom-call(s32[1]{0:T(128)} %bitcast.slab, f32[16,40,256]{2,1,0:T(8,128)S(1)} %bitcast.10, bf16[3,768,256]{2,1,0:T(8,128)(2,1)S(1)} %prepare.1.w_pair), custom_call_target="tpu_custom_call" | custom-call | tf_op jit(solution)/shard_map/second_conv/pallas_call | solution.py:318
  59.5 7.5 %all-to-all-start.1 = ((f32[8,8,8,128]{3,2,1,0:T(8,128)}), f32[8,8,8,128]{3,2,1,0:T(8,128)S(1)}, u32[]{:S(2)}, u32[]{:S(2)}) async-start(f32[8,8,8,128]{3,2,1,0:T(8,128)} %get-tuple-element.31), calls=%async_computation.1 | async-start | bytes 524288 | tf_op jit(solution)/shard_map/all_to_all | solution.py:334
  67.1 4.6 %collective-permute-start.5 = (f32[8,64,128]{2,1,0:T(8,128)S(1)}, f32[8,64,128]{2,1,0:T(8,128)S(1)}, u32[]{:S(2)}, u32[]{:S(2)}) collective-permute-start(f32[8,64,128]{2,1,0:T(8,128)S(1)} %copy-done.1), channel_id=1, source_target_pairs={{0,256},{128,384},{256,0},{384,128},{1,257},{129,385},{257,1},{385... | collective-permute-start | bytes 786440 | tf_op jit(solution)/shard_map/ppermute | solution.py:36
  71.7 1.9 %collective-permute-start.6 = (f32[8,64,128]{2,1,0:T(8,128)S(1)}, f32[8,64,128]{2,1,0:T(8,128)S(1)}, u32[]{:S(2)}, u32[]{:S(2)}) collective-permute-start(f32[8,64,128]{2,1,0:T(8,128)S(1)} %copy-done.1), channel_id=1, source_target_pairs={{0,128},{128,0},{256,384},{384,256},{1,129},{129,1},{257,385},{385... | collective-permute-start | bytes 786440 | tf_op jit(solution)/shard_map/ppermute | solution.py:36
  73.6 3.3 %collective-permute-start.7 = (f32[8,64,128]{2,1,0:T(8,128)S(1)}, f32[8,64,128]{2,1,0:T(8,128)S(1)}, u32[]{:S(2)}, u32[]{:S(2)}) collective-permute-start(f32[8,64,128]{2,1,0:T(8,128)S(1)} %copy-done.1), channel_id=1, source_target_pairs={{0,384},{128,256},{256,128},{384,0},{1,385},{129,257},{257,129},{3... | collective-permute-start | bytes 786440 | tf_op jit(solution)/shard_map/ppermute | solution.py:36
  77.0 4.6 %collective-permute-start.8 = (f32[256,128]{1,0:T(8,128)S(1)}, f32[256,128]{1,0:T(8,128)S(1)}, u32[]{:S(2)}, u32[]{:S(2)}) collective-permute-start(f32[256,128]{1,0:T(8,128)S(1)} %get-tuple-element.28), channel_id=1, source_target_pairs={{0,256},{128,384},{256,0},{384,128},{1,257},{129,385},{257,1},{385... | collective-permute-start | bytes 393224 | tf_op jit(solution)/shard_map/ppermute | solution.py:36
  81.5 1.9 %collective-permute-start.3 = (f32[256,128]{1,0:T(8,128)S(1)}, f32[256,128]{1,0:T(8,128)S(1)}, u32[]{:S(2)}, u32[]{:S(2)}) collective-permute-start(f32[256,128]{1,0:T(8,128)S(1)} %get-tuple-element.25), channel_id=1, source_target_pairs={{0,128},{128,0},{256,384},{384,256},{1,129},{129,1},{257,385},{385... | collective-permute-start | bytes 393224 | tf_op jit(solution)/shard_map/ppermute | solution.py:36
  83.5 3.3 %collective-permute-start.4 = (f32[256,128]{1,0:T(8,128)S(1)}, f32[256,128]{1,0:T(8,128)S(1)}, u32[]{:S(2)}, u32[]{:S(2)}) collective-permute-start(f32[256,128]{1,0:T(8,128)S(1)} %get-tuple-element.26), channel_id=1, source_target_pairs={{0,384},{128,256},{256,128},{384,0},{1,385},{129,257},{257,129},{3... | collective-permute-start | bytes 393224 | tf_op jit(solution)/shard_map/ppermute | solution.py:36
  87.3 0.8 collective-permute-done.8.refs_5_
  88.1 2.4 %early_sums.1 = (f32[3,128,256]{2,1,0:T(8,128)S(1)}, bf16[2,3,256,512]{3,2,1,0:T(8,128)(2,1)S(1)}) custom-call(s32[1]{0:T(128)} %bitcast.slab, f32[8,64,128]{2,1,0:T(8,128)} %refs_0_.1, f32[8,64,128]{2,1,0:T(8,128)} %copy-done.2, f32[8,64,128]{2,1,0:T(8,128)} %copy-done.3, f32[8,64,128]{2,1,0:T(8,128)} %copy-done.4, ...), custom_call_target="tpu_custom_call" | custom-call | tf_op jit(solution)/shard_map/early_sums/pallas_call | solution.py:339
  90.4 1.1 %collective-permute-done.4.refs_1_ = f32[256,128]{1,0:T(8,128)S(1)} collective-permute-done((f32[256,128]{1,0:T(8,128)S(1)}, f32[256,128]{1,0:T(8,128)S(1)}, u32[]{:S(2)}, u32[]{:S(2)}) %collective-permute-start.4) | collective-permute-done | bytes 131104 | tf_op jit(solution)/shard_map/ppermute | solution.py:36
  91.6 1.7 %last_sums.1 = (f32[9,64,128]{2,1,0:T(8,128)}, f32[8,8,128]{2,1,0:T(8,128)}) custom-call(f32[256,128]{1,0:T(8,128)S(1)} %collective-permute-done.3.refs_0_, f32[256,128]{1,0:T(8,128)S(1)} %collective-permute-done.4.refs_1_, bf16[2,3,256,512]{3,2,1,0:T(8,128)(2,1)S(1)} %get-tuple-element.29.refs_2_, f32[3,128,256]{2,1,0:T(8,128)S(1)} %get-tuple-element.30.refs_3_, ...), custom_call_target="tpu_custom_call" | custom-call | tf_op jit(solution)/shard_map/last_sums/pallas_call | solution.py:356
  (20 shorter events, 1.9 us)
Async XLA Ops:
  1.5 6.2 %collective-permute-start = (f32[2,64,128]{2,1,0:T(8,128)S(1)}, f32[2,64,128]{2,1,0:T(8,128)S(1)}, u32[]{:S(2)}, u32[]{:S(2)}) collective-permute-start(f32[2,64,128]{2,1,0:T(8,128)S(1)} %get-tuple-element.35), channel_id=1, source_target_pairs={{0,128},{128,256},{256,384},{1,129},{129,257},{257,385},{2,130},{1... | collective-permute-start | bytes 196616 | tf_op jit(solution)/shard_map/ppermute | solution.py:31
  4.9 6.2 %collective-permute-start.1 = (f32[2,64,128]{2,1,0:T(8,128)S(1)}, f32[2,64,128]{2,1,0:T(8,128)S(1)}, u32[]{:S(2)}, u32[]{:S(2)}) collective-permute-start(f32[2,64,128]{2,1,0:T(8,128)S(1)} %get-tuple-element.34), channel_id=1, source_target_pairs={{128,0},{256,128},{384,256},{129,1},{257,129},{385,257},{130,2},{2... | collective-permute-start | bytes 196616 | tf_op jit(solution)/shard_map/ppermute | solution.py:31
  12.1 3.5 %collective-permute-start.2 = (f32[320,256]{1,0:T(8,128)S(1)}, f32[320,256]{1,0:T(8,128)S(1)}, u32[]{:S(2)}, u32[]{:S(2)}) collective-permute-start(f32[320,256]{1,0:T(8,128)S(1)} %get-tuple-element.24), channel_id=1, source_target_pairs={{0,1},{1,0},{2,3},{3,2},{4,5},{5,4},{6,7},{7,6},{8,9},{9,8},{10,11... | collective-permute-start | bytes 983048 | tf_op jit(solution)/shard_map/ppermute | solution.py:300
  15.0 11.7 %copy-start = (f32[3,3,256,128]{3,2,1,0:T(8,128)S(1)}, f32[3,3,256,128]{3,2,1,0:T(8,128)}, u32[]{:S(2)}) copy-start(f32[3,3,256,128]{3,2,1,0:T(8,128)} %param.6) | copy-start | bytes 3538948
  16.4 23.9 %all-to-all-start = ((f32[8,40,256]{2,1,0:T(8,128)}), f32[8,40,256]{2,1,0:T(8,128)S(1)}, u32[]{:S(2)}, u32[]{:S(2)}) async-start(f32[8,40,256]{2,1,0:T(8,128)} %bitcast.6), calls=%async_computation | async-start | bytes 655360 | tf_op jit(solution)/shard_map/all_to_all | solution.py:301
  57.4 9.7 %copy-start.1 = (f32[8,64,128]{2,1,0:T(8,128)S(1)}, f32[8,64,128]{2,1,0:T(8,128)}, u32[]{:S(2)}) copy-start(f32[8,64,128]{2,1,0:T(8,128)} %refs_0_.1) | copy-start | bytes 786436
  59.5 32.1 %all-to-all-start.1 = ((f32[8,8,8,128]{3,2,1,0:T(8,128)}), f32[8,8,8,128]{3,2,1,0:T(8,128)S(1)}, u32[]{:S(2)}, u32[]{:S(2)}) async-start(f32[8,8,8,128]{3,2,1,0:T(8,128)} %get-tuple-element.31), calls=%async_computation.1 | async-start | bytes 524288 | tf_op jit(solution)/shard_map/all_to_all | solution.py:334
  67.1 16.4 %collective-permute-start.5 = (f32[8,64,128]{2,1,0:T(8,128)S(1)}, f32[8,64,128]{2,1,0:T(8,128)S(1)}, u32[]{:S(2)}, u32[]{:S(2)}) collective-permute-start(f32[8,64,128]{2,1,0:T(8,128)S(1)} %copy-done.1), channel_id=1, source_target_pairs={{0,256},{128,384},{256,0},{384,128},{1,257},{129,385},{257,1},{385... | collective-permute-start | bytes 786440 | tf_op jit(solution)/shard_map/ppermute | solution.py:36
  71.7 15.1 %collective-permute-start.6 = (f32[8,64,128]{2,1,0:T(8,128)S(1)}, f32[8,64,128]{2,1,0:T(8,128)S(1)}, u32[]{:S(2)}, u32[]{:S(2)}) collective-permute-start(f32[8,64,128]{2,1,0:T(8,128)S(1)} %copy-done.1), channel_id=1, source_target_pairs={{0,128},{128,0},{256,384},{384,256},{1,129},{129,1},{257,385},{385... | collective-permute-start | bytes 786440 | tf_op jit(solution)/shard_map/ppermute | solution.py:36
  73.6 13.6 %collective-permute-start.7 = (f32[8,64,128]{2,1,0:T(8,128)S(1)}, f32[8,64,128]{2,1,0:T(8,128)S(1)}, u32[]{:S(2)}, u32[]{:S(2)}) collective-permute-start(f32[8,64,128]{2,1,0:T(8,128)S(1)} %copy-done.1), channel_id=1, source_target_pairs={{0,384},{128,256},{256,128},{384,0},{1,385},{129,257},{257,129},{3... | collective-permute-start | bytes 786440 | tf_op jit(solution)/shard_map/ppermute | solution.py:36
  77.0 11.1 %collective-permute-start.8 = (f32[256,128]{1,0:T(8,128)S(1)}, f32[256,128]{1,0:T(8,128)S(1)}, u32[]{:S(2)}, u32[]{:S(2)}) collective-permute-start(f32[256,128]{1,0:T(8,128)S(1)} %get-tuple-element.28), channel_id=1, source_target_pairs={{0,256},{128,384},{256,0},{384,128},{1,257},{129,385},{257,1},{385... | collective-permute-start | bytes 393224 | tf_op jit(solution)/shard_map/ppermute | solution.py:36
  81.5 8.9 %collective-permute-start.3 = (f32[256,128]{1,0:T(8,128)S(1)}, f32[256,128]{1,0:T(8,128)S(1)}, u32[]{:S(2)}, u32[]{:S(2)}) collective-permute-start(f32[256,128]{1,0:T(8,128)S(1)} %get-tuple-element.25), channel_id=1, source_target_pairs={{0,128},{128,0},{256,384},{384,256},{1,129},{129,1},{257,385},{385... | collective-permute-start | bytes 393224 | tf_op jit(solution)/shard_map/ppermute | solution.py:36
  83.5 4.6 %copy-start.2 = (f32[8,64,128]{2,1,0:T(8,128)}, f32[8,64,128]{2,1,0:T(8,128)S(1)}, u32[]{:S(2)}) copy-start(f32[8,64,128]{2,1,0:T(8,128)S(1)} %collective-permute-done.5.refs_1_) | copy-start | bytes 786436
  83.5 8.1 %collective-permute-start.4 = (f32[256,128]{1,0:T(8,128)S(1)}, f32[256,128]{1,0:T(8,128)S(1)}, u32[]{:S(2)}, u32[]{:S(2)}) collective-permute-start(f32[256,128]{1,0:T(8,128)S(1)} %get-tuple-element.26), channel_id=1, source_target_pairs={{0,384},{128,256},{256,128},{384,0},{1,385},{129,257},{257,129},{3... | collective-permute-start | bytes 393224 | tf_op jit(solution)/shard_map/ppermute | solution.py:36
  86.8 1.2 %copy-start.3 = (f32[8,64,128]{2,1,0:T(8,128)}, f32[8,64,128]{2,1,0:T(8,128)S(1)}, u32[]{:S(2)}) copy-start(f32[8,64,128]{2,1,0:T(8,128)S(1)} %collective-permute-done.6.refs_2_) | copy-start | bytes 786436
  87.2 0.8 copy-start.4

commit v7 on v6

--- a/solution.py
+++ b/solution.py
@@ -226,13 +226,19 @@
             out[a] = value if step == 0 else out[a] + value
 
 
+def middle_sums(cols, source, grad_t, sums, out, high, low):
+    pixel_taps(cols, source, high, low)
+    for a, value in enumerate(pixel_sums(grad_t.at[0], high, low)):
+        out[a] = sums[a] + value
+
+
 def last_sums(cols, *refs):
     *local, grad_t, sums, gathered, out, output, high, low = refs
     part = out.shape[1]
     terms = []
     for step, source in enumerate(local):
         pixel_taps(cols, source, high.at[step], low.at[step])
-        terms.append(pixel_sums(grad_t.at[step], high.at[step], low.at[step]))
+        terms.append(pixel_sums(grad_t.at[step + 1], high.at[step], low.at[step]))
     for a in range(3):
         turned = sum((term[a] for term in terms), sums[a]).T
         for b in range(3):
@@ -353,18 +359,27 @@
         name="early_sums",
         compiler_params=LIMIT,
     )(slab[None], *map(far, grads), *map(near, local[:early]))
+    sums = pl.pallas_call(
+        functools.partial(middle_sums, cols),
+        out_shape=pltpu.VMEM((3, wide, 2 * lanes), F32),
+        in_specs=[VMEM] * 3,
+        out_specs=VMEM,
+        scratch_shapes=[pltpu.VMEM((pixels, 2 * lanes), BF16)] * 2,
+        name="middle_sums",
+        compiler_params=LIMIT,
+    )(*map(near, (local[early], grad_last, sums)))
     weight_grad, output = pl.pallas_call(
         functools.partial(last_sums, cols),
         out_shape=[
             jax.ShapeDtypeStruct((9, mid // slabs, wide), F32),
             jax.ShapeDtypeStruct((rows, cols // n_out, wide), F32),
         ],
-        in_specs=[VMEM] * (slabs - early + 3),
+        in_specs=[VMEM] * (slabs - early + 2),
         out_specs=[VMEM] * 2,
         scratch_shapes=tap_pair,
         name="last_sums",
         compiler_params=LIMIT,
-    )(*map(near, (*local[early:], grad_last, sums, gathered)))
+    )(*map(near, (*local[early + 1 :], grad_last, sums, gathered)))
     weight_grad = weight_grad.reshape(3, 3, mid // slabs, wide)
     return (output, weight_grad)
 

time: 93.9 us -> 93.7 us (level)
  transfers between devices with their start and end apart: 11 -> 11, of which waited for: 6 -> 6; matrix products, arithmetic and copies ran while one was open for 0% -> 0% of each run, Pallas kernels for 5% -> 6%
where the time goes in v7:
time: 93.7 us; the launch traced here: 93 us
  starting transfers between devices  44.2 us (47%)
  waiting for transfers between devices  18.9 us (20%)
  blocking collectives  16.5 us (18%)
  Pallas kernels  10.9 us (12%)
    ppermute x6, starting transfers between devices, trade(): return lax.ppermute(value, axis, [(i, i ^ step) for i in range(count)])  19.7 us
    all_gather x1, blocking collectives, block(): hidden = lax.all_gather(own, ('chip', 'core'), axis=0, tiled=False)  16.5 us
    all_to_all x1, waiting for transfers between devices, block(): lax.all_to_all(held.reshape(chips, chunk, mid), 'chip', 0, 0, tiled=True)  13.3 us
    all_to_all x1, starting transfers between devices, block(): lax.all_to_all(held.reshape(chips, chunk, mid), 'chip', 0, 0, tiled=True)  10.3 us
    all_to_all x1, starting transfers between devices, block(): gathered = lax.all_to_all(conv, 'cout', 0, 0, tiled=True)  7.55 us
    ppermute x2, starting transfers between devices, shift(): return lax.ppermute(value, axis, pairs)  4.69 us
    ppermute x2, waiting for transfers between devices, shift(): return lax.ppermute(value, axis, pairs)  3.32 us
    pallas_call x1, Pallas kernels, block(): pl.pallas_call(functools.partial(early_sums, cols), out_shape=[pltpu.VMEM...  2.37 us
  transfers between devices with their start and end apart: 11, of which 6 were waited for; matrix products, arithmetic and copies ran while one was open for 0% of the time, Pallas kernels for 6%

profile of v7, /device:TPU:8, one launch (start us, length us, event | category | flops | bytes accessed | tf_op | source)
XLA Modules:
  0.0 93.0 jit_solution(1180062666695689084)
XLA Ops:
  0.6 0.9 fusion
  1.5 3.4 %collective-permute-start = (f32[2,64,128]{2,1,0:T(8,128)S(1)}, f32[2,64,128]{2,1,0:T(8,128)S(1)}, u32[]{:S(2)}, u32[]{:S(2)}) collective-permute-start(f32[2,64,128]{2,1,0:T(8,128)S(1)} %get-tuple-element.35), channel_id=1, source_target_pairs={{0,128},{128,256},{256,384},{1,129},{129,257},{257,385},{2,130},{1... | collective-permute-start | bytes 196616 | tf_op jit(solution)/shard_map/ppermute | solution.py:31
  4.9 1.3 %collective-permute-start.1 = (f32[2,64,128]{2,1,0:T(8,128)S(1)}, f32[2,64,128]{2,1,0:T(8,128)S(1)}, u32[]{:S(2)}, u32[]{:S(2)}) collective-permute-start(f32[2,64,128]{2,1,0:T(8,128)S(1)} %get-tuple-element.34), channel_id=1, source_target_pairs={{128,0},{256,128},{384,256},{129,1},{257,129},{385,257},{130,2},{2... | collective-permute-start | bytes 196616 | tf_op jit(solution)/shard_map/ppermute | solution.py:31
  6.2 1.5 %first_prepare.1 = (bf16[512,384]{1,0:T(8,128)(2,1)S(1)}, bf16[512,384]{1,0:T(8,128)(2,1)S(1)}, bf16[3,384,256]{2,1,0:T(8,128)(2,1)S(1)}, bf16[3,384,256]{2,1,0:T(8,128)(2,1)S(1)}) custom-call(f32[8,64,128]{2,1,0:T(8,128)} %image.1, f32[9,128,256]{2,1,0:T(8,128)} %bitcast.12), custom_call_target="tpu_custom_call" | custom-call | tf_op jit(solution)/shard_map/first_prepare/pallas_call | solution.py:267
  7.8 3.3 %collective-permute-done.1.below = f32[2,64,128]{2,1,0:T(8,128)S(1)} collective-permute-done((f32[2,64,128]{2,1,0:T(8,128)S(1)}, f32[2,64,128]{2,1,0:T(8,128)S(1)}, u32[]{:S(2)}, u32[]{:S(2)}) %collective-permute-start.1) | collective-permute-done | bytes 65568 | tf_op jit(solution)/shard_map/ppermute | solution.py:31
  11.1 1.0 %first_given.1 = (f32[320,256]{1,0:T(8,128)S(1)}, bf16[768,384]{1,0:T(8,128)(2,1)S(1)}, bf16[768,384]{1,0:T(8,128)(2,1)S(1)}) custom-call(s32[1]{0:T(128)} %bitcast.4.core, f32[2,64,128]{2,1,0:T(8,128)S(1)} %collective-permute-done.above, f32[2,64,128]{2,1,0:T(8,128)S(1)} %collective-permute-done.1.below, bf16[512,384]{1,0:T(8,128)(2,1)S(1)} %get-tuple-element.18.high_in, ...), custom_call_target="tpu_custom_call" | custom-call | tf_op jit(solution)/shard_map/first_given/pallas_call | solution.py:280
  12.1 1.9 %collective-permute-start.2 = (f32[320,256]{1,0:T(8,128)S(1)}, f32[320,256]{1,0:T(8,128)S(1)}, u32[]{:S(2)}, u32[]{:S(2)}) collective-permute-start(f32[320,256]{1,0:T(8,128)S(1)} %get-tuple-element.24), channel_id=1, source_target_pairs={{0,1},{1,0},{2,3},{3,2},{4,5},{5,4},{6,7},{7,6},{8,9},{9,8},{10,11... | collective-permute-start | bytes 983048 | tf_op jit(solution)/shard_map/ppermute | solution.py:306
  14.0 0.9 first_held.1
  15.6 0.8 add.7
  16.4 10.3 %all-to-all-start = ((f32[8,40,256]{2,1,0:T(8,128)}), f32[8,40,256]{2,1,0:T(8,128)S(1)}, u32[]{:S(2)}, u32[]{:S(2)}) async-start(f32[8,40,256]{2,1,0:T(8,128)} %bitcast.6), calls=%async_computation | async-start | bytes 655360 | tf_op jit(solution)/shard_map/all_to_all | solution.py:307
  27.0 13.3 %all-to-all-done.pieces = f32[8,40,256]{2,1,0:T(8,128)S(1)} async-done(((f32[8,40,256]{2,1,0:T(8,128)}), f32[8,40,256]{2,1,0:T(8,128)S(1)}, u32[]{:S(2)}, u32[]{:S(2)}) %all-to-all-start) | async-done | bytes 327712 | tf_op jit(solution)/shard_map/all_to_all | solution.py:307
  40.9 16.5 %all-gather = f32[640,256]{1,0:T(8,128)S(1)} all-gather(f32[40,256]{1,0:T(8,128)S(1)} %activate.1), channel_id=2, replica_groups=mesh['slab'=4,'cout'=8,'chip'=8,'core'=2] {'chip','core'}, dimensions={0}, use_global_device_ids=true | all-gather | bytes 696320 | tf_op jit(solution)/shard_map/all_gather | solution.py:320
  57.4 2.1 %second_conv.1 = (f32[8,8,8,128]{3,2,1,0:T(8,128)}, f32[256,128]{1,0:T(8,128)S(1)}, f32[256,128]{1,0:T(8,128)S(1)}, f32[256,128]{1,0:T(8,128)S(1)}, f32[256,128]{1,0:T(8,128)S(1)}) custom-call(s32[1]{0:T(128)} %bitcast.slab, f32[16,40,256]{2,1,0:T(8,128)S(1)} %bitcast.10, bf16[3,768,256]{2,1,0:T(8,128)(2,1)S(1)} %prepare.1.w_pair), custom_call_target="tpu_custom_call" | custom-call | tf_op jit(solution)/shard_map/second_conv/pallas_call | solution.py:324
  59.5 7.5 %all-to-all-start.1 = ((f32[8,8,8,128]{3,2,1,0:T(8,128)}), f32[8,8,8,128]{3,2,1,0:T(8,128)S(1)}, u32[]{:S(2)}, u32[]{:S(2)}) async-start(f32[8,8,8,128]{3,2,1,0:T(8,128)} %get-tuple-element.31), calls=%async_computation.1 | async-start | bytes 524288 | tf_op jit(solution)/shard_map/all_to_all | solution.py:340
  67.1 4.6 %collective-permute-start.4 = (f32[8,64,128]{2,1,0:T(8,128)S(1)}, f32[8,64,128]{2,1,0:T(8,128)S(1)}, u32[]{:S(2)}, u32[]{:S(2)}) collective-permute-start(f32[8,64,128]{2,1,0:T(8,128)S(1)} %copy-done.1), channel_id=1, source_target_pairs={{0,256},{128,384},{256,0},{384,128},{1,257},{129,385},{257,1},{385... | collective-permute-start | bytes 786440 | tf_op jit(solution)/shard_map/ppermute | solution.py:36
  71.7 1.9 %collective-permute-start.5 = (f32[8,64,128]{2,1,0:T(8,128)S(1)}, f32[8,64,128]{2,1,0:T(8,128)S(1)}, u32[]{:S(2)}, u32[]{:S(2)}) collective-permute-start(f32[8,64,128]{2,1,0:T(8,128)S(1)} %copy-done.1), channel_id=1, source_target_pairs={{0,128},{128,0},{256,384},{384,256},{1,129},{129,1},{257,385},{385... | collective-permute-start | bytes 786440 | tf_op jit(solution)/shard_map/ppermute | solution.py:36
  73.6 3.3 %collective-permute-start.6 = (f32[8,64,128]{2,1,0:T(8,128)S(1)}, f32[8,64,128]{2,1,0:T(8,128)S(1)}, u32[]{:S(2)}, u32[]{:S(2)}) collective-permute-start(f32[8,64,128]{2,1,0:T(8,128)S(1)} %copy-done.1), channel_id=1, source_target_pairs={{0,384},{128,256},{256,128},{384,0},{1,385},{129,257},{257,129},{3... | collective-permute-start | bytes 786440 | tf_op jit(solution)/shard_map/ppermute | solution.py:36
  77.0 4.6 %collective-permute-start.7 = (f32[256,128]{1,0:T(8,128)S(1)}, f32[256,128]{1,0:T(8,128)S(1)}, u32[]{:S(2)}, u32[]{:S(2)}) collective-permute-start(f32[256,128]{1,0:T(8,128)S(1)} %get-tuple-element.27), channel_id=1, source_target_pairs={{0,256},{128,384},{256,0},{384,128},{1,257},{129,385},{257,1},{385... | collective-permute-start | bytes 393224 | tf_op jit(solution)/shard_map/ppermute | solution.py:36
  81.5 1.9 %collective-permute-start.8 = (f32[256,128]{1,0:T(8,128)S(1)}, f32[256,128]{1,0:T(8,128)S(1)}, u32[]{:S(2)}, u32[]{:S(2)}) collective-permute-start(f32[256,128]{1,0:T(8,128)S(1)} %get-tuple-element.29), channel_id=1, source_target_pairs={{0,128},{128,0},{256,384},{384,256},{1,129},{129,1},{257,385},{385... | collective-permute-start | bytes 393224 | tf_op jit(solution)/shard_map/ppermute | solution.py:36
  83.5 3.3 %collective-permute-start.3 = (f32[256,128]{1,0:T(8,128)S(1)}, f32[256,128]{1,0:T(8,128)S(1)}, u32[]{:S(2)}, u32[]{:S(2)}) collective-permute-start(f32[256,128]{1,0:T(8,128)S(1)} %get-tuple-element.25), channel_id=1, source_target_pairs={{0,384},{128,256},{256,128},{384,0},{1,385},{129,257},{257,129},{3... | collective-permute-start | bytes 393224 | tf_op jit(solution)/shard_map/ppermute | solution.py:36
  87.3 0.8 collective-permute-done.7.refs_5_
  88.1 2.4 %early_sums.1 = (f32[3,128,256]{2,1,0:T(8,128)S(1)}, bf16[2,3,256,512]{3,2,1,0:T(8,128)(2,1)S(1)}) custom-call(s32[1]{0:T(128)} %bitcast.slab, f32[8,64,128]{2,1,0:T(8,128)} %refs_0_.1, f32[8,64,128]{2,1,0:T(8,128)} %copy-done.2, f32[8,64,128]{2,1,0:T(8,128)} %copy-done.3, f32[8,64,128]{2,1,0:T(8,128)} %copy-done.4, ...), custom_call_target="tpu_custom_call" | custom-call | tf_op jit(solution)/shard_map/early_sums/pallas_call | solution.py:345
  90.4 0.7 middle_sums.1.refs_2_
  91.6 1.5 %last_sums.1 = (f32[9,64,128]{2,1,0:T(8,128)}, f32[8,8,128]{2,1,0:T(8,128)}) custom-call(f32[256,128]{1,0:T(8,128)S(1)} %collective-permute-done.3.refs_0_, bf16[2,3,256,512]{3,2,1,0:T(8,128)(2,1)S(1)} %get-tuple-element.28.grad_t.refs_1_, f32[3,128,256]{2,1,0:T(8,128)S(1)} %middle_sums.1.refs_2_, f32[8,8,8,128]{3,2,1,0:T(8,128)S(1)} %all-to-all-done.1.refs_3_), custom_call_target="tpu_custom_call" | custom-call | tf_op jit(solution)/shard_map/last_sums/pallas_call | solution.py:371
  (21 shorter events, 2.4 us)
Async XLA Ops:
  1.5 6.2 %collective-permute-start = (f32[2,64,128]{2,1,0:T(8,128)S(1)}, f32[2,64,128]{2,1,0:T(8,128)S(1)}, u32[]{:S(2)}, u32[]{:S(2)}) collective-permute-start(f32[2,64,128]{2,1,0:T(8,128)S(1)} %get-tuple-element.35), channel_id=1, source_target_pairs={{0,128},{128,256},{256,384},{1,129},{129,257},{257,385},{2,130},{1... | collective-permute-start | bytes 196616 | tf_op jit(solution)/shard_map/ppermute | solution.py:31
  4.9 6.2 %collective-permute-start.1 = (f32[2,64,128]{2,1,0:T(8,128)S(1)}, f32[2,64,128]{2,1,0:T(8,128)S(1)}, u32[]{:S(2)}, u32[]{:S(2)}) collective-permute-start(f32[2,64,128]{2,1,0:T(8,128)S(1)} %get-tuple-element.34), channel_id=1, source_target_pairs={{128,0},{256,128},{384,256},{129,1},{257,129},{385,257},{130,2},{2... | collective-permute-start | bytes 196616 | tf_op jit(solution)/shard_map/ppermute | solution.py:31
  12.1 3.5 %collective-permute-start.2 = (f32[320,256]{1,0:T(8,128)S(1)}, f32[320,256]{1,0:T(8,128)S(1)}, u32[]{:S(2)}, u32[]{:S(2)}) collective-permute-start(f32[320,256]{1,0:T(8,128)S(1)} %get-tuple-element.24), channel_id=1, source_target_pairs={{0,1},{1,0},{2,3},{3,2},{4,5},{5,4},{6,7},{7,6},{8,9},{9,8},{10,11... | collective-permute-start | bytes 983048 | tf_op jit(solution)/shard_map/ppermute | solution.py:306
  15.0 11.7 %copy-start = (f32[3,3,256,128]{3,2,1,0:T(8,128)S(1)}, f32[3,3,256,128]{3,2,1,0:T(8,128)}, u32[]{:S(2)}) copy-start(f32[3,3,256,128]{3,2,1,0:T(8,128)} %param.6) | copy-start | bytes 3538948
  16.4 23.9 %all-to-all-start = ((f32[8,40,256]{2,1,0:T(8,128)}), f32[8,40,256]{2,1,0:T(8,128)S(1)}, u32[]{:S(2)}, u32[]{:S(2)}) async-start(f32[8,40,256]{2,1,0:T(8,128)} %bitcast.6), calls=%async_computation | async-start | bytes 655360 | tf_op jit(solution)/shard_map/all_to_all | solution.py:307
  57.4 9.7 %copy-start.1 = (f32[8,64,128]{2,1,0:T(8,128)S(1)}, f32[8,64,128]{2,1,0:T(8,128)}, u32[]{:S(2)}) copy-start(f32[8,64,128]{2,1,0:T(8,128)} %refs_0_.1) | copy-start | bytes 786436
  59.5 32.1 %all-to-all-start.1 = ((f32[8,8,8,128]{3,2,1,0:T(8,128)}), f32[8,8,8,128]{3,2,1,0:T(8,128)S(1)}, u32[]{:S(2)}, u32[]{:S(2)}) async-start(f32[8,8,8,128]{3,2,1,0:T(8,128)} %get-tuple-element.31), calls=%async_computation.1 | async-start | bytes 524288 | tf_op jit(solution)/shard_map/all_to_all | solution.py:340
  67.1 16.4 %collective-permute-start.4 = (f32[8,64,128]{2,1,0:T(8,128)S(1)}, f32[8,64,128]{2,1,0:T(8,128)S(1)}, u32[]{:S(2)}, u32[]{:S(2)}) collective-permute-start(f32[8,64,128]{2,1,0:T(8,128)S(1)} %copy-done.1), channel_id=1, source_target_pairs={{0,256},{128,384},{256,0},{384,128},{1,257},{129,385},{257,1},{385... | collective-permute-start | bytes 786440 | tf_op jit(solution)/shard_map/ppermute | solution.py:36
  71.7 15.1 %collective-permute-start.5 = (f32[8,64,128]{2,1,0:T(8,128)S(1)}, f32[8,64,128]{2,1,0:T(8,128)S(1)}, u32[]{:S(2)}, u32[]{:S(2)}) collective-permute-start(f32[8,64,128]{2,1,0:T(8,128)S(1)} %copy-done.1), channel_id=1, source_target_pairs={{0,128},{128,0},{256,384},{384,256},{1,129},{129,1},{257,385},{385... | collective-permute-start | bytes 786440 | tf_op jit(solution)/shard_map/ppermute | solution.py:36
  73.6 13.6 %collective-permute-start.6 = (f32[8,64,128]{2,1,0:T(8,128)S(1)}, f32[8,64,128]{2,1,0:T(8,128)S(1)}, u32[]{:S(2)}, u32[]{:S(2)}) collective-permute-start(f32[8,64,128]{2,1,0:T(8,128)S(1)} %copy-done.1), channel_id=1, source_target_pairs={{0,384},{128,256},{256,128},{384,0},{1,385},{129,257},{257,129},{3... | collective-permute-start | bytes 786440 | tf_op jit(solution)/shard_map/ppermute | solution.py:36
  77.0 11.1 %collective-permute-start.7 = (f32[256,128]{1,0:T(8,128)S(1)}, f32[256,128]{1,0:T(8,128)S(1)}, u32[]{:S(2)}, u32[]{:S(2)}) collective-permute-start(f32[256,128]{1,0:T(8,128)S(1)} %get-tuple-element.27), channel_id=1, source_target_pairs={{0,256},{128,384},{256,0},{384,128},{1,257},{129,385},{257,1},{385... | collective-permute-start | bytes 393224 | tf_op jit(solution)/shard_map/ppermute | solution.py:36
  81.5 8.9 %collective-permute-start.8 = (f32[256,128]{1,0:T(8,128)S(1)}, f32[256,128]{1,0:T(8,128)S(1)}, u32[]{:S(2)}, u32[]{:S(2)}) collective-permute-start(f32[256,128]{1,0:T(8,128)S(1)} %get-tuple-element.29), channel_id=1, source_target_pairs={{0,128},{128,0},{256,384},{384,256},{1,129},{129,1},{257,385},{385... | collective-permute-start | bytes 393224 | tf_op jit(solution)/shard_map/ppermute | solution.py:36
  83.5 4.6 %copy-start.2 = (f32[8,64,128]{2,1,0:T(8,128)}, f32[8,64,128]{2,1,0:T(8,128)S(1)}, u32[]{:S(2)}) copy-start(f32[8,64,128]{2,1,0:T(8,128)S(1)} %collective-permute-done.4.refs_1_) | copy-start | bytes 786436
  83.5 8.1 %collective-permute-start.3 = (f32[256,128]{1,0:T(8,128)S(1)}, f32[256,128]{1,0:T(8,128)S(1)}, u32[]{:S(2)}, u32[]{:S(2)}) collective-permute-start(f32[256,128]{1,0:T(8,128)S(1)} %get-tuple-element.25), channel_id=1, source_target_pairs={{0,384},{128,256},{256,128},{384,0},{1,385},{129,257},{257,129},{3... | collective-permute-start | bytes 393224 | tf_op jit(solution)/shard_map/ppermute | solution.py:36
  86.8 1.2 %copy-start.3 = (f32[8,64,128]{2,1,0:T(8,128)}, f32[8,64,128]{2,1,0:T(8,128)S(1)}, u32[]{:S(2)}) copy-start(f32[8,64,128]{2,1,0:T(8,128)S(1)} %collective-permute-done.5.refs_2_) | copy-start | bytes 786436
  87.2 0.8 copy-start.4
